TPU v7x, 32 devices: a whole 2x2x4 slice. The times are simulated.
32 devices in a mesh: dp: 8 (over z, y), mp: 4 (over x, core).
Axes of the slice: x: 2, y: 2, z: 4, core: 2. Of those that a mesh axis runs over, the one named last changes fastest.
Arguments:
- suffix: bfloat16 [3584, 768], P('dp'), may hold values from -6 to 6
- memory: bfloat16 [28672, 768], P('dp'), may hold values from -6 to 6
- cotangent: bfloat16 [3584, 768], P('dp'), may hold values from -6 to 6
- group_kind: int32 [112], P('dp'), may hold values 0 or 1
- prefix_len: int32 [112], P('dp'), may hold values from 1 to 32
- suffix_len: int32 [112], P('dp'), may hold values from 1 to 32
- gain_self: float32 [768], replicated, may hold values from 0.25 to 1.75
- shift_self: float32 [768], replicated, may hold values from -2 to 2
- gain_cross: float32 [768], replicated, may hold values from 0.25 to 1.75
- shift_cross: float32 [768], replicated, may hold values from -2 to 2
- gain_mlp: float32 [768], replicated, may hold values from 0.25 to 1.75
- shift_mlp: float32 [768], replicated, may hold values from -2 to 2
- self_query: bfloat16 [768, 768], P(None, 'mp'), may hold values from -0.21875 to 0.21875
- self_key: bfloat16 [768, 768], P(None, 'mp'), may hold values from -0.21875 to 0.21875
- self_value: bfloat16 [768, 768], P(None, 'mp'), may hold values from -0.21875 to 0.21875
- self_out: bfloat16 [768, 768], P('mp'), may hold values from -0.875 to 0.875
- cross_query: bfloat16 [768, 768], P(None, 'mp'), may hold values from -0.21875 to 0.21875
- cross_key: bfloat16 [768, 768], P(None, 'mp'), may hold values from -0.21875 to 0.21875
- cross_value: bfloat16 [768, 768], P(None, 'mp'), may hold values from -0.21875 to 0.21875
- cross_out: bfloat16 [768, 768], P('mp'), may hold values from -1.75 to 1.75
- mlp_up: bfloat16 [768, 3072], P(None, 'mp'), may hold values from -0.21875 to 0.21875
- mlp_down: bfloat16 [3072, 768], P('mp'), may hold values from -0.109375 to 0.109375
Outputs:
- layer_out: bfloat16 [3584, 768], P('dp')
- suffix_grad: bfloat16 [3584, 768], P('dp')
- memory_grad: bfloat16 [28672, 768], P('dp')
- grad_self_query: float32 [768, 768], P('dp', 'mp')
- grad_self_key: float32 [768, 768], P('dp', 'mp')
- grad_self_value: float32 [768, 768], P('dp', 'mp')
- grad_self_out: float32 [768, 768], P('mp', 'dp')
- grad_cross_query: float32 [768, 768], P('dp', 'mp')
- grad_cross_key: float32 [768, 768], P('dp', 'mp')
- grad_cross_value: float32 [768, 768], P('dp', 'mp')
- grad_cross_out: float32 [768, 768], P('mp', 'dp')
- grad_mlp_up: float32 [768, 3072], P('dp', 'mp')
- grad_mlp_down: float32 [3072, 768], P('mp', 'dp')
- grad_gain_self: float32 [768], P('dp')
- grad_shift_self: float32 [768], P('dp')
- grad_gain_cross: float32 [768], P('dp')
- grad_shift_cross: float32 [768], P('dp')
- grad_gain_mlp: float32 [768], P('dp')
- grad_shift_mlp: float32 [768], P('dp')
Inputs may be any that keep to these rules, and one draw needn't show every extreme that they name: `group_kind`: 1 marks an image-text group, whose memory holds 196 patches and then its prefix; 0 a text-only group, whose memory holds its prefix only. memory slot j of a group is live when j < 196 * group_kind + prefix_len. suffix positions at or past suffix_len are padding and are never attended to.
All inputs are finite; a program needn't handle non-finite values.
Results may differ from a plain program's by a relative error of at most 0.019.
Values may be sent and summed in bfloat16 or wider, within the bound.
A program may use at most 128 MiB of HBM per device.

v0:
```python
import math

import jax
import jax.numpy as jnp
from jax import lax
from jax.sharding import PartitionSpec as P

HEAD_DIM = 64
SUFFIX = 32
PATCHES = 196
MEM = 256


EPSILON = 1e-06
NEG_FILL = -1e30


def matmul(left_side, right_side):
    return jnp.dot(left_side, right_side, preferred_element_type=jnp.float32)


def matmul_tn(left_side, right_side):
    return lax.dot_general(
        left_side, right_side, (((0,), (0,)), ((), ())), preferred_element_type=jnp.float32
    )


def matmul_nt(left_side, right_side):
    return lax.dot_general(
        left_side, right_side, (((1,), (1,)), ((), ())), preferred_element_type=jnp.float32
    )


def normalize(vector):
    centred = vector - jnp.mean(vector, axis=-1, keepdims=True)
    inverse = lax.rsqrt(jnp.mean(centred * centred, axis=-1, keepdims=True) + EPSILON)
    return (centred * inverse, inverse)


def norm_back(unit_part, inverse, gain_row, incoming):
    scaled = incoming * gain_row
    return inverse * (
        scaled
        - jnp.mean(scaled, axis=-1, keepdims=True)
        - unit_part * jnp.mean(scaled * unit_part, axis=-1, keepdims=True)
    )


def gelu_exact(vector):
    return jax.nn.gelu(vector, approximate=False)


def build_masks(group_kinds, prefixes, lengths):
    places = jnp.arange(SUFFIX)
    memory_slots = jnp.arange(MEM)
    self_mask = (places[None, :, None] >= places[None, None, :]) & (
        places[None, None, :] < lengths[:, None, None]
    )
    reach_len = group_kinds * PATCHES + prefixes
    cross_mask = memory_slots[None, None, :] < reach_len[:, None, None]
    return (self_mask, cross_mask)


def split_heads(matrix, groups):
    return matrix.reshape(groups, -1, matrix.shape[1] // HEAD_DIM, HEAD_DIM)


def masked_scores(query_heads, key_heads, allowed, factor):
    scores = (
        jnp.einsum("gqhe,gkhe->ghqk", query_heads, key_heads, preferred_element_type=jnp.float32)
        * factor
    )
    return jnp.where(allowed[:, None], scores, NEG_FILL)


def attend_forward(queries, keys_in, values_in, allowed, factor):
    groups = allowed.shape[0]
    scores = masked_scores(
        split_heads(queries, groups), split_heads(keys_in, groups), allowed, factor
    )
    highest = jnp.max(scores, axis=-1, keepdims=True)
    total_log = highest + jnp.log(jnp.sum(jnp.exp(scores - highest), axis=-1, keepdims=True))
    weights = jnp.exp(scores - total_log).astype(jnp.bfloat16)
    mixed_out = jnp.einsum(
        "ghqk,gkhe->gqhe",
        weights,
        split_heads(values_in, groups),
        preferred_element_type=jnp.float32,
    )
    return (mixed_out.reshape(queries.shape).astype(jnp.bfloat16), total_log)


def attend_backward(queries, keys_in, values_in, allowed, factor, total_log, grad_mixed):
    groups = allowed.shape[0]
    query_heads = split_heads(queries, groups)
    key_heads = split_heads(keys_in, groups)
    value_heads = split_heads(values_in, groups)
    grad_heads = split_heads(grad_mixed, groups)
    weights_full = jnp.exp(masked_scores(query_heads, key_heads, allowed, factor) - total_log)
    weights = weights_full.astype(jnp.bfloat16)
    grad_values = jnp.einsum(
        "ghqk,gqhe->gkhe", weights, grad_heads, preferred_element_type=jnp.float32
    )
    grad_weights = jnp.einsum(
        "gqhe,gkhe->ghqk", grad_heads, value_heads, preferred_element_type=jnp.float32
    )
    centre = jnp.sum(weights_full * grad_weights, axis=-1, keepdims=True)
    grad_scores = (weights_full * (grad_weights - centre)).astype(jnp.bfloat16)
    grad_queries = (
        jnp.einsum("ghqk,gkhe->gqhe", grad_scores, key_heads, preferred_element_type=jnp.float32)
        * factor
    )
    grad_keys = (
        jnp.einsum("ghqk,gqhe->gkhe", grad_scores, query_heads, preferred_element_type=jnp.float32)
        * factor
    )
    return (
        grad_queries.reshape(queries.shape).astype(jnp.bfloat16),
        grad_keys.reshape(keys_in.shape).astype(jnp.bfloat16),
        grad_values.reshape(values_in.shape).astype(jnp.bfloat16),
    )


def on_device(
    suffix,
    memory,
    cotangent,
    group_kind,
    prefix_len,
    suffix_len,
    gain_self,
    shift_self,
    gain_cross,
    shift_cross,
    gain_mlp,
    shift_mlp,
    self_query,
    self_key,
    self_value,
    self_out,
    cross_query,
    cross_key,
    cross_value,
    cross_out,
    mlp_up,
    mlp_down,
):
    factor = 1.0 / math.sqrt(HEAD_DIM)
    self_mask, cross_mask = build_masks(group_kind, prefix_len, suffix_len)
    inputs = suffix.astype(jnp.float32)
    unit_one, inverse_one = normalize(inputs)
    normed_one = (unit_one * gain_self + shift_self).astype(jnp.bfloat16)
    query_one = matmul(normed_one, self_query).astype(jnp.bfloat16)
    key_one = matmul(normed_one, self_key).astype(jnp.bfloat16)
    value_one = matmul(normed_one, self_value).astype(jnp.bfloat16)
    mixed_one, log_one = attend_forward(query_one, key_one, value_one, self_mask, factor)
    hidden_one = inputs + lax.psum(matmul(mixed_one, self_out), "mp")
    unit_two, inverse_two = normalize(hidden_one)
    normed_two = (unit_two * gain_cross + shift_cross).astype(jnp.bfloat16)
    query_two = matmul(normed_two, cross_query).astype(jnp.bfloat16)
    key_two = matmul(memory, cross_key).astype(jnp.bfloat16)
    value_two = matmul(memory, cross_value).astype(jnp.bfloat16)
    mixed_two, log_two = attend_forward(query_two, key_two, value_two, cross_mask, factor)
    hidden_two = hidden_one + lax.psum(matmul(mixed_two, cross_out), "mp")
    unit_three, inverse_three = normalize(hidden_two)
    normed_three = (unit_three * gain_mlp + shift_mlp).astype(jnp.bfloat16)
    pre_act = matmul(normed_three, mlp_up)
    act_value, act_back = jax.vjp(gelu_exact, pre_act)
    activated = act_value.astype(jnp.bfloat16)
    layer_out = (
        hidden_two
        + lax.psum(matmul(activated, mlp_down).astype(jnp.bfloat16), "mp").astype(jnp.float32)
    ).astype(jnp.bfloat16)
    grad_down = matmul_tn(activated, cotangent)
    grad_act = matmul_nt(cotangent, mlp_down)
    grad_pre = act_back(grad_act)[0].astype(jnp.bfloat16)
    grad_up = matmul_tn(normed_three, grad_pre)
    back_three = lax.psum(matmul_nt(grad_pre, mlp_up), "mp")
    gain_mlp_grad = jnp.sum(back_three * unit_three, axis=0)
    shift_mlp_grad = jnp.sum(back_three, axis=0)
    grad_two = cotangent.astype(jnp.float32) + norm_back(
        unit_three, inverse_three, gain_mlp, back_three
    )
    carry_two = grad_two.astype(jnp.bfloat16)
    grad_cross_out = matmul_tn(mixed_two, carry_two)
    mixed_grad_two = matmul_nt(carry_two, cross_out).astype(jnp.bfloat16)
    query_grad_two, key_grad_two, value_grad_two = attend_backward(
        query_two, key_two, value_two, cross_mask, factor, log_two, mixed_grad_two
    )
    grad_cross_query = matmul_tn(normed_two, query_grad_two)
    grad_cross_key = matmul_tn(memory, key_grad_two)
    grad_cross_value = matmul_tn(memory, value_grad_two)
    part_suffix = matmul_nt(query_grad_two, cross_query)
    part_memory = matmul_nt(key_grad_two, cross_key) + matmul_nt(value_grad_two, cross_value)
    back_two, memory_total = lax.psum((part_suffix, part_memory), "mp")
    memory_grad = memory_total.astype(jnp.bfloat16)
    gain_cross_grad = jnp.sum(back_two * unit_two, axis=0)
    shift_cross_grad = jnp.sum(back_two, axis=0)
    grad_one = grad_two + norm_back(unit_two, inverse_two, gain_cross, back_two)
    carry_one = grad_one.astype(jnp.bfloat16)
    grad_self_out_part = matmul_tn(mixed_one, carry_one)
    mixed_grad_one = matmul_nt(carry_one, self_out).astype(jnp.bfloat16)
    query_grad_one, key_grad_one, value_grad_one = attend_backward(
        query_one, key_one, value_one, self_mask, factor, log_one, mixed_grad_one
    )
    grad_self_query_part = matmul_tn(normed_one, query_grad_one)
    grad_self_key_part = matmul_tn(normed_one, key_grad_one)
    grad_self_value_part = matmul_tn(normed_one, value_grad_one)
    part_self = (
        matmul_nt(query_grad_one, self_query)
        + matmul_nt(key_grad_one, self_key)
        + matmul_nt(value_grad_one, self_value)
    )
    back_one = lax.psum(part_self, "mp")
    gain_self_grad = jnp.sum(back_one * unit_one, axis=0)
    shift_self_grad = jnp.sum(back_one, axis=0)
    suffix_grad = (grad_one + norm_back(unit_one, inverse_one, gain_self, back_one)).astype(
        jnp.bfloat16
    )
    (
        grad_self_query,
        grad_self_key,
        grad_self_value,
        grad_self_out,
        grad_gain_self,
        grad_shift_self,
        grad_mlp_up,
        grad_mlp_down,
        grad_gain_mlp,
        grad_shift_mlp,
        grad_cross_query_sum,
        grad_cross_key_sum,
        grad_cross_value_sum,
        grad_cross_out_sum,
        grad_gain_cross,
        grad_shift_cross,
    ) = (
        lax.psum_scatter(grad_self_query_part, "dp", scatter_dimension=0, tiled=True),
        lax.psum_scatter(grad_self_key_part, "dp", scatter_dimension=0, tiled=True),
        lax.psum_scatter(grad_self_value_part, "dp", scatter_dimension=0, tiled=True),
        lax.psum_scatter(grad_self_out_part, "dp", scatter_dimension=1, tiled=True),
        lax.psum_scatter(gain_self_grad, "dp", scatter_dimension=0, tiled=True),
        lax.psum_scatter(shift_self_grad, "dp", scatter_dimension=0, tiled=True),
        lax.psum_scatter(grad_up, "dp", scatter_dimension=0, tiled=True),
        lax.psum_scatter(grad_down, "dp", scatter_dimension=1, tiled=True),
        lax.psum_scatter(gain_mlp_grad, "dp", scatter_dimension=0, tiled=True),
        lax.psum_scatter(shift_mlp_grad, "dp", scatter_dimension=0, tiled=True),
        lax.psum_scatter(grad_cross_query, "dp", scatter_dimension=0, tiled=True),
        lax.psum_scatter(grad_cross_key, "dp", scatter_dimension=0, tiled=True),
        lax.psum_scatter(grad_cross_value, "dp", scatter_dimension=0, tiled=True),
        lax.psum_scatter(grad_cross_out, "dp", scatter_dimension=1, tiled=True),
        lax.psum_scatter(gain_cross_grad, "dp", scatter_dimension=0, tiled=True),
        lax.psum_scatter(shift_cross_grad, "dp", scatter_dimension=0, tiled=True),
    )
    return (
        layer_out,
        suffix_grad,
        memory_grad,
        grad_self_query,
        grad_self_key,
        grad_self_value,
        grad_self_out,
        grad_cross_query_sum,
        grad_cross_key_sum,
        grad_cross_value_sum,
        grad_cross_out_sum,
        grad_mlp_up,
        grad_mlp_down,
        grad_gain_self,
        grad_shift_self,
        grad_gain_cross,
        grad_shift_cross,
        grad_gain_mlp,
        grad_shift_mlp,
    )


def solution(mesh):
    in_specs = (
        P("dp", None),
        P("dp", None),
        P("dp", None),
        P("dp"),
        P("dp"),
        P("dp"),
        P(),
        P(),
        P(),
        P(),
        P(),
        P(),
        P(None, "mp"),
        P(None, "mp"),
        P(None, "mp"),
        P("mp", None),
        P(None, "mp"),
        P(None, "mp"),
        P(None, "mp"),
        P("mp", None),
        P(None, "mp"),
        P("mp", None),
    )
    out_specs = (
        P("dp", None),
        P("dp", None),
        P("dp", None),
        P("dp", "mp"),
        P("dp", "mp"),
        P("dp", "mp"),
        P("mp", "dp"),
        P("dp", "mp"),
        P("dp", "mp"),
        P("dp", "mp"),
        P("mp", "dp"),
        P("dp", "mp"),
        P("mp", "dp"),
        P("dp"),
        P("dp"),
        P("dp"),
        P("dp"),
        P("dp"),
        P("dp"),
    )
    return jax.shard_map(
        on_device, mesh=mesh, in_specs=in_specs, out_specs=out_specs, check_vma=False
    )
```

profile of v0, /device:TPU:0, one launch (start us, length us, event | category | flops | bytes accessed | tf_op | source)
XLA Modules:
  0.0 1003.9 jit_solution(15678607943310992722)
XLA Ops:
  22.4 4.5 convolution_convert_fusion
  28.8 4.8 convolution_convert_fusion.1
  35.7 28.9 %all-reduce.15.cloned.1.call-done = f32[448,768]{1,0:T(8,128)} async-done(((f32[448,768]{1,0:T(8,128)}), f32[448,768]{1,0:T(8,128)}) %all-reduce.15.cloned.1.call-update) | async-done | bytes 1376272 | tf_op jit(solution)/shard_map/psum | solution.py:157
  81.3 39.8 %all-reduce.17.cloned.1.call-done = f32[448,768]{1,0:T(8,128)} async-done(((f32[448,768]{1,0:T(8,128)}), f32[448,768]{1,0:T(8,128)}) %all-reduce.17.cloned.1.call-update) | async-done | bytes 1376272 | tf_op jit(solution)/shard_map/psum | solution.py:164
  125.6 4.8 add_convert_fusion
  137.7 35.5 %all-reduce.21.cloned.1.call-done = f32[448,768]{1,0:T(8,128)} async-done(((f32[448,768]{1,0:T(8,128)}), f32[448,768]{1,0:T(8,128)}) %all-reduce.21.cloned.1.call-update) | async-done | bytes 1376272 | tf_op jit(solution)/shard_map/psum | solution.py:178
  173.2 3.0 multiply_reduce_fusion
  176.2 34.0 %all-reduce.19.cloned.1.call-done = bf16[448,768]{1,0:T(8,128)(2,1)} async-done(((bf16[448,768]{1,0:T(8,128)(2,1)}), bf16[448,768]{1,0:T(8,128)(2,1)}) %all-reduce.19.cloned.1.call-update) | async-done | bytes 688144 | tf_op jit(solution)/shard_map/psum | solution.py:172
  210.2 3.3 multiply_add_fusion.1
  216.3 3.0 multiply_reduce_fusion.3
  227.7 36.9 %all-reduce.23.cloned.1.call-done = f32[448,768]{1,0:T(8,128)} async-done(((f32[448,768]{1,0:T(8,128)}), f32[448,768]{1,0:T(8,128)}) %all-reduce.23.cloned.1.call-update) | async-done | bytes 1376272 | tf_op jit(solution)/shard_map/psum | solution.py:195
  286.5 3.9 convolution_bitcast_fusion.3
  295.3 3.8 convolution_bitcast_fusion.2
  314.8 5.9 convolution_add_fusion
  320.7 212.3 %all-reduce.26 = bf16[3584,768]{1,0:T(8,128)(2,1)} all-reduce(f32[3584,768]{1,0:T(8,128)} %convolution_add_fusion), channel_id=1, replica_groups=mesh['dp'=8,'mp'=4] {'mp'}, use_global_device_ids=true, to_apply=%region_24.25 | all-reduce | flops 2752512 | bytes 16515072 | tf_op jit(solution)/shard_map/psum | solution.py:195
  536.8 37.6 %all-reduce.6 = (f32[768]{0:T(1024)S(1)}, f32[768]{0:T(1024)S(1)}, f32[768]{0:T(1024)S(1)}, f32[768]{0:T(1024)S(1)}, f32[768]{0:T(1024)S(1)}, /*index=5*/f32[768]{0:T(1024)S(1)}) all-reduce(f32[768]{0:T(1024)S(1)} %get-tuple-element.80, f32[768]{0:T(1024)S(1)} %get-tuple-element.87, ...), channel_id=12, replica_groups=mesh['dp'=8,'mp'=4] {'dp'}, use_global_device_ids=true, to_apply=%region_36.37.clone | all-reduce | flops 4608 | bytes 36864
  577.9 2.8 fusion.15
  582.4 8.9 reduce-scatter.33.cloned.1.call-done
  591.3 65.3 %reduce-scatter.35.cloned.1.call-done = f32[96,192]{1,0:T(8,128)} async-done(((f32[768,192]{1,0:T(8,128)}), f32[96,192]{1,0:T(8,128)}) %reduce-scatter.35.cloned.1.call-update) | async-done | bytes 73744
  656.6 65.5 %reduce-scatter.23.cloned.1.call-done = f32[96,192]{1,0:T(8,128)} async-done(((f32[768,192]{1,0:T(8,128)}), f32[96,192]{1,0:T(8,128)}) %reduce-scatter.23.cloned.1.call-update) | async-done | bytes 73744 | tf_op jit(solution)/shard_map/reduce_scatter | solution.py:240
  722.1 65.4 %reduce-scatter.21.cloned.1.call-done = f32[96,192]{1,0:T(8,128)} async-done(((f32[768,192]{1,0:T(8,128)}), f32[96,192]{1,0:T(8,128)}) %reduce-scatter.21.cloned.1.call-update) | async-done | bytes 73744 | tf_op jit(solution)/shard_map/reduce_scatter | solution.py:239
  787.5 65.6 %reduce-scatter.19.cloned.1.call-done = f32[96,192]{1,0:T(8,128)} async-done(((f32[768,192]{1,0:T(8,128)}), f32[96,192]{1,0:T(8,128)}) %reduce-scatter.19.cloned.1.call-update) | async-done | bytes 73744 | tf_op jit(solution)/shard_map/reduce_scatter | solution.py:238
  853.0 71.8 %reduce-scatter.27.cloned.1.call-done = f32[96,768]{1,0:T(8,128)} async-done(((f32[768,768]{1,0:T(8,128)}), f32[96,768]{1,0:T(8,128)}) %reduce-scatter.27.cloned.1.call-update) | async-done | bytes 294928 | tf_op jit(solution)/shard_map/reduce_scatter | solution.py:244
  924.9 72.0 %reduce-scatter.29.cloned.1.call-done = f32[768,96]{0,1:T(8,128)} async-done(((f32[768,768]{0,1:T(8,128)}), f32[768,96]{0,1:T(8,128)}) %reduce-scatter.29.cloned.1.call-update) | async-done | bytes 294928 | tf_op jit(solution)/shard_map/reduce_scatter | solution.py:245
  (308 shorter events, 108.3 us)
Async XLA Ops:
  7.2 118.2 %copy-start = (bf16[768,768]{1,0:T(8,128)(2,1)S(1)}, bf16[768,768]{1,0:T(8,128)(2,1)}, u32[]{:S(2)}) copy-start(bf16[768,768]{1,0:T(8,128)(2,1)} %param.43) | copy-start | bytes 3538948
  7.2 57.3 %all-reduce.15.cloned.1.call-start = ((), (), s32[]{:S(2)}) async-start(), calls=%async_computation.10 | async-start | bytes 2752512 | tf_op jit(solution)/shard_map/psum | solution.py:157
  21.8 99.3 %all-reduce.17.cloned.1.call-start = ((), (), s32[]{:S(2)}) async-start(), calls=%async_computation.11 | async-start | bytes 2752512 | tf_op jit(solution)/shard_map/psum | solution.py:164
  81.1 92.1 %all-reduce.21.cloned.1.call-start = ((), (), s32[]{:S(2)}) async-start(), calls=%async_computation.13 | async-start | bytes 2752512 | tf_op jit(solution)/shard_map/psum | solution.py:178
  133.2 77.0 %all-reduce.19.cloned.1.call-start = ((), (), s32[]{:S(2)}) async-start(), calls=%async_computation.12 | async-start | bytes 1376256 | tf_op jit(solution)/shard_map/psum | solution.py:172
  137.6 72.6 %copy-start.36 = (bf16[448,768]{1,0:T(8,128)(2,1)S(1)}, bf16[448,768]{1,0:T(8,128)(2,1)}, u32[]{:S(2)}) copy-start(bf16[448,768]{1,0:T(8,128)(2,1)} %param.24) | copy-start | bytes 2064388
  137.6 72.6 %copy-start.64 = (f32[448]{0:T(512)S(1)}, f32[448]{0:T(512)}, u32[]{:S(2)}) copy-start(f32[448]{0:T(512)} %copy-done.63) | copy-start | bytes 5380
  137.6 72.6 %copy-start.69 = (f32[768]{0:T(1024)S(1)}, f32[768]{0:T(1024)}, u32[]{:S(2)}) copy-start(f32[768]{0:T(1024)} %param.32) | copy-start | bytes 9220
  137.6 127.0 %all-reduce.23.cloned.1.call-start = ((), (), s32[]{:S(2)}) async-start(), calls=%async_computation.14 | async-start | bytes 2752512 | tf_op jit(solution)/shard_map/psum | solution.py:195
  224.7 40.0 %copy-start.62 = (f32[448]{0:T(512)S(1)}, f32[448]{0:T(512)}, u32[]{:S(2)}) copy-start(f32[448]{0:T(512)} %copy-done.61) | copy-start | bytes 5380
  224.7 308.3 %reduce-scatter.37.cloned.1.call-start = ((), (), s32[]{:S(2)}) async-start(), calls=%async_computation.25 | async-start | bytes 884736
  227.4 307.3 %all-reduce.25.cloned.1.call-start = ((), (), s32[]{:S(2)}) async-start(), calls=%async_computation.15 | async-start | bytes 2752512 | tf_op jit(solution)/shard_map/psum | solution.py:214
  278.3 302.5 %reduce-scatter.31.cloned.1.call-start = ((), (), s32[]{:S(2)}) async-start(), calls=%async_computation.22 | async-start | bytes 884736
  280.9 301.4 %reduce-scatter.25.cloned.1.call-start = ((), (), s32[]{:S(2)}) async-start(), calls=%async_computation.19 | async-start | bytes 884736 | tf_op jit(solution)/shard_map/reduce_scatter | solution.py:248
  283.4 307.9 %reduce-scatter.33.cloned.1.call-start = ((), (), s32[]{:S(2)}) async-start(), calls=%async_computation.23 | async-start | bytes 884736
  291.6 365.0 %reduce-scatter.35.cloned.1.call-start = ((), (), s32[]{:S(2)}) async-start(), calls=%async_computation.24 | async-start | bytes 884736
  300.4 421.7 %reduce-scatter.23.cloned.1.call-start = ((), (), s32[]{:S(2)}) async-start(), calls=%async_computation.18 | async-start | bytes 884736 | tf_op jit(solution)/shard_map/reduce_scatter | solution.py:240
  301.9 485.6 %reduce-scatter.21.cloned.1.call-start = ((), (), s32[]{:S(2)}) async-start(), calls=%async_computation.17 | async-start | bytes 884736 | tf_op jit(solution)/shard_map/reduce_scatter | solution.py:239
  303.3 549.7 %reduce-scatter.19.cloned.1.call-start = ((), (), s32[]{:S(2)}) async-start(), calls=%async_computation.16 | async-start | bytes 884736 | tf_op jit(solution)/shard_map/reduce_scatter | solution.py:238
  304.8 620.1 %reduce-scatter.27.cloned.1.call-start = ((), (), s32[]{:S(2)}) async-start(), calls=%async_computation.20 | async-start | bytes 2654208 | tf_op jit(solution)/shard_map/reduce_scatter | solution.py:244
  307.6 689.3 %reduce-scatter.29.cloned.1.call-start = ((), (), s32[]{:S(2)}) async-start(), calls=%async_computation.21 | async-start | bytes 2654208 | tf_op jit(solution)/shard_map/reduce_scatter | solution.py:245
  320.7 214.1 %copy-start.6 = (bf16[448,768]{1,0:T(8,128)(2,1)S(1)}, bf16[448,768]{1,0:T(8,128)(2,1)}, u32[]{:S(2)}) copy-start(bf16[448,768]{1,0:T(8,128)(2,1)} %param.22) | copy-start | bytes 2064388
  533.0 44.9 %copy-start.13 = (f32[448,768]{1,0:T(8,128)S(1)}, f32[448,768]{1,0:T(8,128)}, u32[]{:S(2)}) copy-start(f32[448,768]{1,0:T(8,128)} %copy-done.11) | copy-start | bytes 4128772
  577.9 419.0 %copy-start.1 = (bf16[768,768]{1,0:T(8,128)(2,1)S(1)}, bf16[768,768]{1,0:T(8,128)(2,1)}, u32[]{:S(2)}) copy-start(bf16[768,768]{1,0:T(8,128)(2,1)} %param.43) | copy-start | bytes 3538948
  (73 other events, 130.8 us)
Sparse Core Ops, SparseCore 0:
  21.9 42.5 all-reduce.14
  81.2 39.8 all-reduce.16
  133.3 39.8 all-reduce.20
  176.1 34.0 all-reduce.18
  224.8 39.8 all-reduce.22
  268.2 62.4 reduce-scatter.36
  333.1 61.0 all-reduce.24
  397.8 62.5 reduce-scatter.30
  464.2 61.4 reduce-scatter.24
  529.8 61.3 reduce-scatter.32
  595.1 61.4 reduce-scatter.34
  660.7 61.3 reduce-scatter.22
  726.0 61.4 reduce-scatter.20
  791.5 61.4 reduce-scatter.18
  856.9 67.8 reduce-scatter.26
  928.8 68.0 reduce-scatter.28
where the time goes:
time: 1010 us; the launch traced here: 1000 us
  waiting for transfers between devices  590 us (58%)
  blocking collectives  250 us (25%)
  matrix products  70.3 us (7%)
  local copies, waits for them, and re-layouts  49 us (5%)
  other arithmetic  26.8 us (3%)
  between operations  16.2 us (2%)
    psum x1, blocking collectives, on_device(): back_two, memory_total = lax.psum((part_suffix, part_memory), 'mp')  212 us
    unnamed x20, waiting for transfers between devices  74.5 us
    reduce_scatter x1, waiting for transfers between devices, on_device(): lax.psum_scatter(grad_down, 'dp', scatter_dimension=1, tiled=True)  72 us
    reduce_scatter x1, waiting for transfers between devices, on_device(): lax.psum_scatter(grad_up, 'dp', scatter_dimension=0, tiled=True)  71.8 us
    reduce_scatter x1, waiting for transfers between devices, on_device(): lax.psum_scatter(grad_self_query_part, 'dp', scatter_dimension=0, tiled=T...  65.6 us
    reduce_scatter x1, waiting for transfers between devices, on_device(): lax.psum_scatter(grad_self_value_part, 'dp', scatter_dimension=0, tiled=T...  65.5 us
    reduce_scatter x1, waiting for transfers between devices, on_device(): lax.psum_scatter(grad_self_key_part, 'dp', scatter_dimension=0, tiled=True)  65.4 us
    psum x1, waiting for transfers between devices, on_device(): hidden_two = hidden_one + lax.psum(matmul(mixed_two, cross_out), 'mp')  39.8 us
  transfers between devices with their start and end apart: 16, of which 12 were waited for; matrix products, arithmetic and copies ran while one was open for 8% of the time, Pallas kernels for 0%

commit v1 on v0

v1 whole, which is shorter than its diff:
```python
import math

import jax
import jax.numpy as jnp
from jax import lax
from jax.experimental import pallas as pl
from jax.experimental.pallas import tpu as pltpu
from jax.sharding import PartitionSpec as P

BF = jnp.bfloat16
F32 = jnp.float32
MESH = pl.DeviceIdType.MESH
HEAD = 64
PATCHES = 196
EPSILON = 1e-06
NEG_FILL = -1e30
UNIT = 384
ROWS = 32
N_SEMS = 160


def nn(a, b):
    return lax.dot_general(a, b, (((1,), (0,)), ((), ())), preferred_element_type=F32)


def nt(a, b):
    return lax.dot_general(a, b, (((1,), (1,)), ((), ())), preferred_element_type=F32)


def tn(a, b):
    return lax.dot_general(a, b, (((0,), (0,)), ((), ())), preferred_element_type=F32)


def normalize(v):
    centred = v - jnp.mean(v, axis=-1, keepdims=True)
    inverse = lax.rsqrt(jnp.mean(centred * centred, axis=-1, keepdims=True) + EPSILON)
    return centred * inverse, inverse


def norm_back(unit, inverse, gain, incoming):
    w = incoming * gain
    return inverse * (
        w - jnp.mean(w, axis=-1, keepdims=True) - unit * jnp.mean(w * unit, axis=-1, keepdims=True)
    )


def softmax(s):
    p = jnp.exp(s - jnp.max(s, axis=-1, keepdims=True))
    return p * (1.0 / jnp.sum(p, axis=-1, keepdims=True))


def fold8(v):
    total = v[0:8]
    for k in range(8, v.shape[0], 8):
        total = total + v[k : k + 8]
    return total


class Dims:
    def __init__(self, n_dp, n_mp, suffix, memory, group_kind, self_query, mlp_up):
        assert n_mp == 4
        self.n_dp = n_dp
        self.T, self.D = suffix.shape
        self.M = memory.shape[0]
        self.G = group_kind.shape[0]
        self.C = self_query.shape[1]
        self.F = mlp_up.shape[1]
        self.H = n_mp * self.C
        self.S = self.T // self.G
        self.K = self.M // self.G
        self.GO, self.RO, self.MO = self.G // 2, self.T // 2, self.M // 2
        self.NB = self.H // 256
        self.BLK = pl.cdiv(self.T, 128)
        self.TP = self.BLK * 128
        self.bits = n_dp.bit_length() - 1
        assert 1 << self.bits == n_dp
        halvings = 0
        while halvings < self.bits and (self.D >> (halvings + 1)) % 16 == 0:
            halvings += 1
        self.halvings = halvings
        self.low = self.bits - halvings
        self.nch = 1 << halvings
        self.rp = self.D // self.nch


UNITS = ("d1", "d2", "u1", "u2", "s1", "s2", "c1", "c2")
IN_NAMES = (
    "suffix",
    "memory",
    "cotangent",
    "kind",
    "prefix",
    "slen",
    "gain_self",
    "shift_self",
    "gain_cross",
    "shift_cross",
    "gain_mlp",
    "shift_mlp",
    "self_query",
    "self_key",
    "self_value",
    "self_out",
    "cross_query",
    "cross_key",
    "cross_value",
    "cross_out",
    "mlp_up",
    "mlp_down",
)
OUT_NAMES = (
    "layer_out",
    "suffix_grad",
    "memory_grad",
    "g_sq",
    "g_sk",
    "g_sv",
    "g_so",
    "g_cq",
    "g_ck",
    "g_cv",
    "g_co",
    "g_up",
    "g_dn",
    "norms",
)


def scratch(d):
    s = {}
    T, D, C, F, H, RO, MO, K = d.T, d.D, d.C, d.F, d.H, d.RO, d.MO, d.K

    def vmem(name, shape, dtype=BF):
        s[name] = pltpu.VMEM(shape, dtype)

    vmem("xin", (T, D))
    vmem("cot", (T, D))
    vmem("mem", (MO, D))
    for n in ("raw_sq", "raw_sk", "raw_sv", "raw_cq", "raw_ck", "raw_cv"):
        vmem(n, (D, C))
    vmem("wqkv", (D, 3 * C))
    vmem("so", (C, D))
    for n in ("cq", "ck", "cv", "co"):
        vmem(n, (H, D))
    vmem("up", (D, F))
    vmem("dn", (F, D))
    vmem("a1", (T, D))
    for n in ("q1", "k1", "v1", "o1", "do1"):
        vmem(n, (d.TP, C))
    vmem("p1", (d.BLK, 3 * 128, 128))
    vmem("dqkv", (d.TP, 3 * C))
    for k in (1, 3, 4, 6):
        for n in ("s", "r", "xs", "xr"):
            vmem(f"{n}{k}", (RO, D))
    vmem("h1", (RO, D), F32)
    vmem("h2", (RO, D), F32)
    vmem("dh", (RO, D), F32)
    vmem("tmp", (RO, D), F32)
    vmem("a2", (RO, D))
    vmem("c2", (RO, D))
    for n in ("q2", "o2", "do2", "dq2"):
        vmem(n, (RO, H))
    for n in ("k2", "v2", "dk2", "dv2"):
        vmem(n, (MO, H))
    for n in ("p2", "ds2"):
        vmem(n, (d.GO * d.NB, 4 * d.S, K))
    vmem("a3", (T, D))
    vmem("c1", (T, D))
    vmem("act", (T, F))
    vmem("du", (T, F))
    vmem("dact", (T, F), F32)
    vmem("mg", (d.GO, K, D))
    vmem("lo", (RO, D))
    vmem("sg", (RO, D))
    for n in ("cs1", "cs2", "cr1", "cr2"):
        vmem(n, (d.nch, d.rp, UNIT))
    for u in UNITS:
        vmem("g_" + u + "_acc", (d.nch, d.rp, UNIT))
        for k in range(d.halvings):
            vmem(f"g_{u}_r{k}", (d.nch >> (k + 1), d.rp, UNIT))
        for k in range(d.low):
            vmem(f"g_{u}_x{k}", (d.rp, UNIT))
            vmem(f"g_{u}_y{k}", (d.rp, UNIT))
    vmem("nst", (2 + d.bits, 8, D), F32)
    vmem("nrc", (1 + d.bits, 8, D), F32)
    s["ss"] = pltpu.SemaphoreType.DMA((N_SEMS,))
    s["rs"] = pltpu.SemaphoreType.DMA((N_SEMS,))
    s["ls"] = pltpu.SemaphoreType.DMA((48,))
    return s


class Refs:
    pass


def kernel(d, names, *args):
    r = Refs()
    for name, ref in zip(names, args):
        setattr(r, name, ref)
    dp, mp = lax.axis_index("dp"), lax.axis_index("mp")
    core = lax.rem(mp, 2)
    sib = {"mp": mp + 1 - 2 * core}
    xmate = {"mp": lax.rem(mp + 2, 4)}
    own = pl.multiple_of(core * d.RO, 16)
    other = pl.multiple_of((1 - core) * d.RO, 16)
    own_rows, other_rows = pl.ds(own, d.RO), pl.ds(other, d.RO)
    factor = 1.0 / math.sqrt(HEAD)

    def bit_of(b):
        return lax.rem(dp // (1 << b), 2)

    def mate(b):
        return {"dp": dp + (1 << b) * (1 - 2 * bit_of(b))}

    state = {"r": 0, "l": 0}
    sends, locals_ = [], []

    def remote(src, dst, device, index=None):
        if index is None:
            index = state["r"]
            state["r"] += 1
        cp = pltpu.make_async_remote_copy(
            src_ref=src,
            dst_ref=dst,
            send_sem=r.ss.at[index],
            recv_sem=r.rs.at[index],
            device_id=device,
            device_id_type=MESH,
        )
        return cp

    def send(src, dst, device):
        cp = remote(src, dst, device)
        cp.start()
        sends.append(cp)
        return cp

    def load(src, dst):
        cp = pltpu.make_async_copy(src, dst, r.ls.at[state["l"]])
        state["l"] += 1
        cp.start()
        return cp

    ld = {}
    mp_rows = pl.ds(pl.multiple_of(mp * d.C, 16), d.C)
    ld["ck"] = load(r.cross_key, r.raw_ck)
    ld["cv"] = load(r.cross_value, r.raw_cv)
    ld["cq"] = load(r.cross_query, r.raw_cq)
    ld["co"] = load(r.cross_out, r.co.at[mp_rows])
    ld["xin"] = load(r.suffix, r.xin)
    ld["sq"] = load(r.self_query, r.raw_sq)
    ld["sk"] = load(r.self_key, r.raw_sk)
    ld["sv"] = load(r.self_value, r.raw_sv)
    ld["so"] = load(r.self_out, r.so)
    ld["cot"] = load(r.cotangent, r.cot)
    ld["dn"] = load(r.mlp_down, r.dn)
    ld["mem"] = load(r.memory.at[pl.ds(pl.multiple_of(core * d.MO, 16), d.MO)], r.mem)
    ld["up"] = load(r.mlp_up, r.up)

    barrier = pltpu.get_barrier_semaphore()
    mates = [sib, xmate] + [mate(b) for b in range(d.bits)]
    for device in mates:
        pl.semaphore_signal(barrier, inc=1, device_id=device, device_id_type=MESH)
    pl.semaphore_wait(barrier, len(mates))

    PC = d.C // 2
    piece = lax.rem(dp, 2)
    full = {"ck": r.ck, "cv": r.cv, "cq": r.cq, "co": r.co}
    raw = {"ck": r.raw_ck, "cv": r.raw_cv, "cq": r.raw_cq}
    xm = lax.rem(mp + 2, 4)
    gat = {}

    def part(ref, owner, which):
        return ref.at[pl.ds(pl.multiple_of(owner * d.C + which * PC, 16), PC)]

    def gather_start(w):
        ref = full[w]
        ld[w].wait()
        if w in raw:
            ref[mp_rows, :] = raw[w][...].T
        mine = part(ref, mp, piece)
        gat[w, "x"] = send(mine, mine, xmate)
        gat[w, "s"] = send(ref.at[mp_rows], ref.at[mp_rows], sib)

    def gather_x(w):
        gat[w, "x"].wait_recv()
        got = part(full[w], xm, piece)
        gat[w, "y"] = send(got, got, mate(0))
        gat[w, "sx"] = send(got, got, sib)

    def gather_y(w):
        gat[w, "y"].wait_recv()
        got = part(full[w], xm, 1 - piece)
        gat[w, "sy"] = send(got, got, sib)

    def gather_done(w):
        for k in ("s", "sx", "sy"):
            gat[w, k].wait_recv()

    for w in ("ck", "cv", "cq", "co"):
        gather_start(w)

    class Unit:
        def __init__(self, name, finish):
            self.name, self.finish, self.stage = name, finish, 0
            self.acc = getattr(r, f"g_{name}_acc")
            self.base = 0
            self.cp = None

        def store(self, value, lane):
            width = value.shape[1]
            for j in range(d.nch):
                p = sum(((j >> k) & 1) * (d.nch >> (k + 1)) for k in range(d.halvings))
                self.acc[p, :, lane : lane + width] = value[j * d.rp : (j + 1) * d.rp].astype(BF)

        def go(self):
            k = self.stage
            if k < d.halvings:
                half = d.nch >> (k + 1)
                b = d.low + k
                dst = getattr(r, f"g_{self.name}_r{k}")
                src = self.acc.at[pl.ds(self.base + (1 - bit_of(b)) * half, half)]
                self.cp = send(src, dst, mate(b))
            else:
                e = k - d.halvings
                x = getattr(r, f"g_{self.name}_x{e}")
                x[...] = self.value.astype(BF)
                self.cp = send(x, getattr(r, f"g_{self.name}_y{e}"), mate(e))

        def step(self):
            k = self.stage
            self.cp.wait_recv()
            if k < d.halvings:
                half = d.nch >> (k + 1)
                got = getattr(r, f"g_{self.name}_r{k}")
                base = self.base + bit_of(d.low + k) * half
                self.base = base
                if k < d.halvings - 1:
                    for j in range(half):
                        self.acc[base + j] = (
                            self.acc[base + j].astype(F32) + got[j].astype(F32)
                        ).astype(BF)
                else:
                    self.value = self.acc[base].astype(F32) + got[0].astype(F32)
            else:
                e = k - d.halvings
                x = getattr(r, f"g_{self.name}_x{e}")
                y = getattr(r, f"g_{self.name}_y{e}")
                self.value = x[...].astype(F32) + y[...].astype(F32)
            self.stage += 1
            if self.stage < d.bits:
                self.go()
            else:
                self.finish(self.value)

        def drain(self):
            while self.stage < d.bits:
                self.step()

    def fin_dn(lane):
        def f(v):
            r.g_dn[lane : lane + UNIT, :] = v.T

        return f

    def fin_up(lane):
        def f(v):
            r.g_up[:, lane : lane + UNIT] = v

        return f

    def fin_pair(left, right, turn):
        def f(v):
            left[...] = v[:, : d.C]
            right[...] = v[:, d.C :].T if turn else v[:, d.C :]

        return f

    units = {
        "d1": Unit("d1", fin_dn(0)),
        "d2": Unit("d2", fin_dn(UNIT)),
        "u1": Unit("u1", fin_up(0)),
        "u2": Unit("u2", fin_up(UNIT)),
        "s1": Unit("s1", fin_pair(r.g_sq, r.g_sk, False)),
        "s2": Unit("s2", fin_pair(r.g_sv, r.g_so, True)),
        "c1": Unit("c1", fin_pair(r.g_cq, r.g_co, True)),
        "c2": Unit("c2", fin_pair(r.g_ck, r.g_cv, False)),
    }

    def steps(*which):
        for u in which:
            if units[u].stage < d.bits:
                units[u].step()

    def reduce_rows(k, partial):
        s, got, xs, xr = (getattr(r, f"{n}{k}") for n in ("s", "r", "xs", "xr"))
        s[...] = partial(other_rows).astype(BF)
        cp = send(s, got, sib)
        value = partial(own_rows)
        cp.wait_recv()
        xs[...] = (value + got[...].astype(F32)).astype(BF)
        return send(xs, xr, xmate)

    def total(k, s):
        return getattr(r, f"xs{k}")[s, :].astype(F32) + getattr(r, f"xr{k}")[s, :].astype(F32)

    def row_loop(n, body, carry=0):
        def step(i, c):
            return body(pl.multiple_of(i * ROWS, ROWS), c)

        return lax.fori_loop(0, n // ROWS, step, carry)

    def vec(ref):
        return ref[...].reshape(1, d.D)

    def head_masks(width, count):
        col = lax.broadcasted_iota(jnp.int32, (1, width), 1)
        f = [((col >= HEAD * h) & (col < HEAD * h + HEAD)).astype(F32) for h in range(count)]
        return f, [m.astype(BF) for m in f]

    HC = d.C // HEAD
    hf1, hb1 = head_masks(d.C, HC)
    hf2, hb2 = head_masks(256, 4)

    def spread(v, masks):
        return jnp.concatenate([v * m for m in masks], axis=0)

    def gatherh(v, masks):
        n = v.shape[0] // len(masks)
        out = v[:n] * masks[0]
        for h in range(1, len(masks)):
            out = out + v[h * n : (h + 1) * n] * masks[h]
        return out

    for n in ("q1", "k1", "v1", "o1", "do1"):
        ref = getattr(r, n)
        ref[d.T :, :] = jnp.zeros((d.TP - d.T, d.C), BF)
    ld["xin"].wait()
    gain, shift = vec(r.gain_self), vec(r.shift_self)

    def norm_one(i, c):
        s = pl.ds(i, ROWS)
        z, _ = normalize(r.xin[s, :].astype(F32))
        r.a1[s, :] = (z * gain + shift).astype(BF)
        return c

    row_loop(d.T, norm_one)
    for k, n in enumerate(("sq", "sk", "sv")):
        ld[n].wait()
        r.wqkv[:, k * d.C : (k + 1) * d.C] = getattr(r, "raw_" + n)[...]
    qkv = nn(r.a1[...], r.wqkv[...])
    r.q1[: d.T, :] = (qkv[:, : d.C] * factor).astype(BF)
    r.k1[: d.T, :] = qkv[:, d.C : 2 * d.C].astype(BF)
    r.v1[: d.T, :] = qkv[:, 2 * d.C :].astype(BF)
    gather_x("ck")

    ri = lax.broadcasted_iota(jnp.int32, (128, 128), 0)
    ci = lax.broadcasted_iota(jnp.int32, (128, 128), 1)
    near = (jnp.right_shift(ri, 5) == jnp.right_shift(ci, 5)) & (ci <= ri)
    place = jnp.bitwise_and(ci, 31)
    per = 128 // d.S
    for t in range(d.BLK):
        lens = jnp.zeros((128, 128), jnp.int32)
        for k in range(per):
            g = t * per + k
            if g < d.G:
                lens = jnp.where(jnp.right_shift(ci, 5) == k, r.slen[g], lens)
        ok = near & (place < lens)
        b = pl.ds(t * 128, 128)
        scores = nt(spread(r.q1[b, :], hb1), r.k1[b, :])
        scores = jnp.concatenate(
            [jnp.where(ok, scores[h * 128 : (h + 1) * 128], NEG_FILL) for h in range(HC)], axis=0
        )
        p = softmax(scores).astype(BF)
        r.p1[t] = p
        r.o1[b, :] = gatherh(nn(p, r.v1[b, :]), hf1).astype(BF)
    gather_x("cv")
    ld["so"].wait()
    x1 = reduce_rows(1, lambda s: nn(r.o1[s, :], r.so[...]))
    gather_x("cq")
    gather_y("ck")

    ld["cot"].wait()
    ld["dn"].wait()
    r.dact[...] = nt(r.cot[...], r.dn[...])
    gather_y("cv")
    gather_x("co")
    ld["mem"].wait()
    gather_done("ck")
    big = d.MO // 4

    def project(w, dst):
        def body(i, c):
            s = pl.ds(pl.multiple_of(i * big, 16), big)
            dst[s, :] = nt(r.mem[s, :], w[...]).astype(BF)
            return c

        lax.fori_loop(0, 4, body, 0)

    project(r.ck, r.k2)
    gather_y("cq")
    gather_done("cv")
    project(r.cv, r.v2)
    gather_y("co")

    x1.wait_recv()
    gain, shift = vec(r.gain_cross), vec(r.shift_cross)

    def norm_two(i, c):
        s = pl.ds(i, ROWS)
        h1 = r.xin[pl.ds(pl.multiple_of(own + i, 16), ROWS), :].astype(F32) + total(1, s)
        r.h1[s, :] = h1
        z, _ = normalize(h1)
        r.a2[s, :] = (z * gain + shift).astype(BF)
        return c

    row_loop(d.RO, norm_two)
    gather_done("cq")
    r.q2[...] = (nt(r.a2[...], r.cq[...]) * factor).astype(BF)
    slot = lax.broadcasted_iota(jnp.int32, (4 * d.S, d.K), 1)

    def cross_forward(g, c):
        n = core * d.GO + g
        live = r.kind[n] * PATCHES + r.prefix[n]
        qs = pl.ds(pl.multiple_of(g * d.S, d.S), d.S)
        ks = pl.ds(pl.multiple_of(g * d.K, d.K), d.K)
        for b in range(d.NB):
            lanes = slice(256 * b, 256 * b + 256)
            scores = nt(spread(r.q2[qs, lanes], hb2), r.k2[ks, lanes])
            p = softmax(jnp.where(slot < live, scores, NEG_FILL)).astype(BF)
            r.p2[g * d.NB + b] = p
            r.o2[qs, lanes] = gatherh(nn(p, r.v2[ks, lanes]), hf2).astype(BF)
        return c

    lax.fori_loop(0, d.GO, cross_forward, 0)
    gather_done("co")
    r.tmp[...] = nn(r.o2[...], r.co[...])
    gain, shift = vec(r.gain_mlp), vec(r.shift_mlp)

    def norm_three(i, c):
        s = pl.ds(i, ROWS)
        h2 = r.h1[s, :] + r.tmp[s, :]
        r.h2[s, :] = h2
        z, _ = normalize(h2)
        r.a3[pl.ds(pl.multiple_of(own + i, 16), ROWS), :] = (z * gain + shift).astype(BF)
        return c

    row_loop(d.RO, norm_three)
    a3 = send(r.a3.at[own_rows], r.a3.at[own_rows], sib)

    ld["up"].wait()
    root = 1.0 / math.sqrt(2.0)
    bell = 1.0 / math.sqrt(2.0 * math.pi)

    def hidden(start):
        r.tmp[...] = nn(r.a3[pl.ds(start, d.RO), :], r.up[...])

        def body(i, c):
            u = r.tmp[pl.ds(i, ROWS), :]
            s = pl.ds(pl.multiple_of(start + i, 16), ROWS)
            half = 0.5 * (1.0 + lax.erf(u * root))
            r.act[s, :] = (u * half).astype(BF)
            slope = half + u * (bell * jnp.exp(-0.5 * u * u))
            r.du[s, :] = (r.dact[s, :] * slope).astype(BF)
            return c

        row_loop(d.RO, body)

    hidden(own)
    a3.wait_recv()
    hidden(other)
    x4 = reduce_rows(4, lambda s: nt(r.du[s, :], r.up[...]))
    for u, lane in (("d1", 0), ("d2", UNIT)):
        units[u].store(tn(r.cot[...], r.act[:, lane : lane + UNIT]), 0)
        units[u].go()
    for u, lane in (("u1", 0), ("u2", UNIT)):
        units[u].store(tn(r.a3[...], r.du[:, lane : lane + UNIT]), 0)
        units[u].go()
    x3 = reduce_rows(3, lambda s: nn(r.act[s, :], r.dn[...]))

    x4.wait_recv()
    gain = vec(r.gain_mlp)
    zero8 = jnp.zeros((8, d.D), F32)

    def back_three(i, c):
        gg, gs = c
        s = pl.ds(i, ROWS)
        e = total(4, s)
        z, inv = normalize(r.h2[s, :])
        dh = r.cot[pl.ds(pl.multiple_of(own + i, 16), ROWS), :].astype(F32) + norm_back(
            z, inv, gain, e
        )
        r.dh[s, :] = dh
        r.c2[s, :] = dh.astype(BF)
        return gg + fold8(e * z), gs + fold8(e)

    gain_mlp_grad, shift_mlp_grad = row_loop(d.RO, back_three, (zero8, zero8))
    r.do2[...] = nt(r.c2[...], r.co[...]).astype(BF)

    def cross_backward(g, c):
        qs = pl.ds(pl.multiple_of(g * d.S, d.S), d.S)
        ks = pl.ds(pl.multiple_of(g * d.K, d.K), d.K)
        for b in range(d.NB):
            lanes = slice(256 * b, 256 * b + 256)
            dp_ = nt(spread(r.do2[qs, lanes], hb2), r.v2[ks, lanes])
            p = r.p2[g * d.NB + b].astype(F32)
            t = p * dp_
            ds = (t - p * jnp.sum(t, axis=-1, keepdims=True)).astype(BF)
            r.ds2[g * d.NB + b] = ds
            r.dq2[qs, lanes] = (gatherh(nn(ds, r.k2[ks, lanes]), hf2) * factor).astype(BF)
        return c

    lax.fori_loop(0, d.GO, cross_backward, 0)
    r.tmp[...] = nn(r.dq2[...], r.cq[...])
    gain = vec(r.gain_cross)

    def back_two(i, c):
        gg, gs = c
        s = pl.ds(i, ROWS)
        e = r.tmp[s, :]
        z, inv = normalize(r.h1[s, :])
        dh = r.dh[s, :] + norm_back(z, inv, gain, e)
        r.dh[s, :] = dh
        r.c1[pl.ds(pl.multiple_of(own + i, 16), ROWS), :] = dh.astype(BF)
        return gg + fold8(e * z), gs + fold8(e)

    gain_cross_grad, shift_cross_grad = row_loop(d.RO, back_two, (zero8, zero8))
    c1 = send(r.c1.at[own_rows], r.c1.at[own_rows], sib)
    steps("d1", "d2")

    r.do1[own_rows, :] = nt(r.c1[own_rows, :], r.so[...]).astype(BF)
    c1.wait_recv()
    r.do1[other_rows, :] = nt(r.c1[other_rows, :], r.so[...]).astype(BF)
    for t in range(d.BLK):
        b = pl.ds(t * 128, 128)
        dom = spread(r.do1[b, :], hb1)
        dp_ = nt(dom, r.v1[b, :])
        pb = r.p1[t]
        p = pb.astype(F32)
        tt = p * dp_
        ds = (tt - p * jnp.sum(tt, axis=-1, keepdims=True)).astype(BF)
        dq = gatherh(nn(ds, r.k1[b, :]), hf1) * factor
        dk = tn(ds, spread(r.q1[b, :], hb1))
        dv = tn(pb, dom)
        r.dqkv[b, : d.C] = dq.astype(BF)
        r.dqkv[b, d.C : 2 * d.C] = dk.astype(BF)
        r.dqkv[b, 2 * d.C :] = dv.astype(BF)
    x6 = reduce_rows(6, lambda s: nt(r.dqkv[s, :], r.wqkv[...]))
    rows = slice(0, d.T)
    units["s1"].store(tn(r.a1[...], r.dqkv[rows, : 2 * d.C]), 0)
    units["s1"].go()
    units["s2"].store(tn(r.a1[...], r.dqkv[rows, 2 * d.C :]), 0)
    units["s2"].store(tn(r.c1[...], r.o1[rows, :]), d.C)
    units["s2"].go()
    steps("u1", "u2", "d1", "d2")

    def cross_keys(g, c):
        qs = pl.ds(pl.multiple_of(g * d.S, d.S), d.S)
        ks = pl.ds(pl.multiple_of(g * d.K, d.K), d.K)
        for b in range(d.NB):
            lanes = slice(256 * b, 256 * b + 256)
            j = g * d.NB + b
            r.dk2[ks, lanes] = tn(r.ds2[j], spread(r.q2[qs, lanes], hb2)).astype(BF)
            r.dv2[ks, lanes] = tn(r.p2[j], spread(r.do2[qs, lanes], hb2)).astype(BF)
        return c

    lax.fori_loop(0, d.GO, cross_keys, 0)
    pair = pl.ds(pl.multiple_of((mp // 2) * 2 * d.C, 128), 2 * d.C)

    def split_columns(unit, away, lane, value):
        left, right = value[:, : d.C], value[:, d.C :]
        first = core == 0
        unit.store(jnp.where(first, left, right), lane)
        away.store(jnp.where(first, right, left), lane)

    class Away:
        def __init__(self, ref):
            self.acc = ref

        store = Unit.store

    away1, away2 = Away(r.cs1), Away(r.cs2)
    split_columns(units["c1"], away1, 0, tn(r.a2[...], r.dq2[:, pair]))
    split_columns(units["c1"], away1, d.C, tn(r.c2[...], r.o2[:, pair]))
    cc1 = send(r.cs1, r.cr1, sib)
    split_columns(units["c2"], away2, 0, tn(r.mem[...], r.dk2[:, pair]))

    def merge(unit, cp, got):
        cp.wait_recv()
        for j in range(d.nch):
            unit.acc[j] = (unit.acc[j].astype(F32) + got[j].astype(F32)).astype(BF)
        unit.go()

    merge(units["c1"], cc1, r.cr1)
    split_columns(units["c2"], away2, d.C, tn(r.mem[...], r.dv2[:, pair]))
    cc2 = send(r.cs2, r.cr2, sib)
    steps("u1", "u2")

    x3.wait_recv()

    def finish_out(i, c):
        s = pl.ds(i, ROWS)
        r.lo[s, :] = (r.h2[s, :] + total(3, s)).astype(BF)
        return c

    row_loop(d.RO, finish_out)
    tail = [send(r.lo, r.layer_out.at[own_rows], sib)]
    locals_.append(load(r.lo, r.layer_out.at[own_rows]))
    merge(units["c2"], cc2, r.cr2)

    x6.wait_recv()
    gain = vec(r.gain_self)

    def back_one(i, c):
        gg, gs = c
        s = pl.ds(i, ROWS)
        e = total(6, s)
        z, inv = normalize(r.xin[pl.ds(pl.multiple_of(own + i, 16), ROWS), :].astype(F32))
        r.sg[s, :] = (r.dh[s, :] + norm_back(z, inv, gain, e)).astype(BF)
        return gg + fold8(e * z), gs + fold8(e)

    gain_self_grad, shift_self_grad = row_loop(d.RO, back_one, (zero8, zero8))
    tail.append(send(r.sg, r.suffix_grad.at[own_rows], sib))
    locals_.append(load(r.sg, r.suffix_grad.at[own_rows]))
    for k, v in enumerate(
        (
            gain_self_grad,
            shift_self_grad,
            gain_cross_grad,
            shift_cross_grad,
            gain_mlp_grad,
            shift_mlp_grad,
        )
    ):
        r.nst[0, k : k + 1, :] = jnp.sum(v, axis=0, keepdims=True)
    r.nst[0, 6:8, :] = jnp.zeros((2, d.D), F32)
    devices = [sib] + [mate(b) for b in range(d.bits)]
    ncp = send(r.nst.at[0], r.nrc.at[0], devices[0])

    def norm_step(k, cp):
        cp.wait_recv()
        r.nst[k + 1] = r.nst[k] + r.nrc[k]
        if k + 1 < len(devices):
            return send(r.nst.at[k + 1], r.nrc.at[k + 1], devices[k + 1])
        return None

    base_r, base_l = state["r"], state["l"]
    state["r"] += d.GO
    state["l"] += d.GO

    def memory_copies(g):
        rows = pl.ds(pl.multiple_of(core * d.MO + g * d.K, 16), d.K)
        there = remote(r.mg.at[g], r.memory_grad.at[rows], sib, base_r + g)
        here = pltpu.make_async_copy(r.mg.at[g], r.memory_grad.at[rows], r.ls.at[base_l + g])
        return there, here

    def memory_group(g, c):
        ks = pl.ds(pl.multiple_of(g * d.K, d.K), d.K)
        value = nn(r.dk2[ks, :], r.ck[...]) + nn(r.dv2[ks, :], r.cv[...])
        r.mg[g] = value.astype(BF)
        there, here = memory_copies(g)
        there.start()
        here.start()
        return c

    lax.fori_loop(0, d.GO, memory_group, 0)
    ncp = norm_step(0, ncp)
    steps("s1", "s2", "d1", "d2")
    k = 1
    while ncp is not None:
        ncp = norm_step(k, ncp)
        k += 1
        if k == 2:
            steps("c1", "c2")
        if k == 3:
            steps("s1", "s2")
    r.norms[...] = r.nst[len(devices)]
    order = ("d1", "d2", "u1", "u2", "s1", "s2", "c1", "c2")
    while any(units[u].stage < d.bits for u in order):
        for u in order:
            if units[u].stage < d.bits:
                units[u].step()
    for g in range(d.GO):
        there, here = memory_copies(g)
        there.wait_recv()
        there.wait_send()
        here.wait()
    for cp in locals_:
        cp.wait()
    for cp in tail:
        cp.wait_recv()
    for cp in sends:
        cp.wait_send()
    assert state["r"] <= N_SEMS


def solution(mesh):
    n_dp, n_mp = mesh.shape["dp"], mesh.shape["mp"]

    def on_device(*args):
        d = Dims(n_dp, n_mp, args[0], args[1], args[3], args[12], args[20])
        assert d.C * 2 == UNIT and d.F == 2 * UNIT
        scr = scratch(d)
        names = IN_NAMES + OUT_NAMES + tuple(scr)
        col, turned = (d.rp, d.C), (d.C, d.rp)
        shapes = [
            ((d.T, d.D), BF),
            ((d.T, d.D), BF),
            ((d.M, d.D), BF),
            (col, F32),
            (col, F32),
            (col, F32),
            (turned, F32),
            (col, F32),
            (col, F32),
            (col, F32),
            (turned, F32),
            ((d.rp, d.F), F32),
            ((d.F, d.rp), F32),
            ((8, d.D), F32),
        ]
        hbm, vmem = pl.BlockSpec(memory_space=pl.ANY), pl.BlockSpec(memory_space=pltpu.VMEM)
        smem = pl.BlockSpec(memory_space=pltpu.SMEM)

        def body(*refs):
            kernel(d, names, *refs)

        outs = pl.pallas_call(
            body,
            out_shape=[jax.ShapeDtypeStruct(*s) for s in shapes],
            in_specs=[hbm] * 3 + [smem] * 3 + [vmem] * 6 + [hbm] * 10,
            out_specs=[hbm] * 3 + [vmem] * 11,
            scratch_shapes=list(scr.values()),
            compiler_params=pltpu.CompilerParams(
                collective_id=0, has_side_effects=True, vmem_limit_bytes=67043328
            ),
            name="layer",
        )(*args)
        big, grads, norms = outs[:3], list(outs[3:13]), outs[13]
        dp = lax.axis_index("dp")
        rows = d.D // n_dp
        if d.low:
            start = lax.rem(dp, 1 << d.low) * rows
            for k, turn in enumerate((0, 0, 0, 1, 0, 0, 0, 1, 0, 1)):
                grads[k] = lax.dynamic_slice_in_dim(grads[k], start, rows, axis=turn)
        vectors = [lax.dynamic_slice_in_dim(norms[k], dp * rows, rows, axis=0) for k in range(6)]
        return (*big, *grads, *vectors)

    row, col, turn = P("dp", None), P("dp", "mp"), P("mp", "dp")
    wide, tall = P(None, "mp"), P("mp", None)
    in_specs = (row,) * 3 + (P("dp"),) * 3 + (P(),) * 6
    in_specs += (wide, wide, wide, tall, wide, wide, wide, tall, wide, tall)
    out_specs = (row,) * 3 + (col, col, col, turn, col, col, col, turn, col, turn)
    out_specs += (P("dp"),) * 6
    return jax.shard_map(
        on_device, mesh=mesh, in_specs=in_specs, out_specs=out_specs, check_vma=False
    )
```

time: 1010 us -> 156 us (0.15)
  waiting for transfers between devices: 590 us -> 0 us
  blocking collectives: 250 us -> 0 us
  Pallas kernels: 0 us -> 124 us
  matrix products: 70.3 us -> 0 us
  other arithmetic: 26.8 us -> 0 us
  local copies, waits for them, and re-layouts: 49 us -> 31.2 us
  between operations: 16.2 us -> 0.73 us
    reduce_scatter x6 -> x0, waiting for transfers between devices: 340 us -> none  [the longest x1 72 us: on_device(): lax.psum_scatter(grad_down, 'dp', scatter_dimension=1, tiled=True)]
    psum x1 -> x0, blocking collectives: 212 us -> none  [on_device(): back_two, memory_total = lax.psum((part_suffix, part_memory), 'mp')]
    psum x6 -> x0, waiting for transfers between devices: 175 us -> none  [the longest x1 39.8 us: on_device(): hidden_two = hidden_one + lax.psum(matmul(mixed_two, cross_out), 'mp')]
    pallas_call x0 -> x1, Pallas kernels: none -> 124 us  [on_device(): pl.pallas_call(body, out_shape=[jax.ShapeDtypeStruct(*s) for s in shapes]...]
    unnamed x20 -> x0, waiting for transfers between devices: 74.5 us -> none
    dot_general x40 -> x0, matrix products: 66.3 us -> none  [the longest x10 19.5 us: matmul_nt(): lax.dot_general(left_side, right_side, (((1,), (1,)), ((), ())), preferre...]
    unnamed x1 -> x0, blocking collectives: 37.6 us -> none
    reshape x14 -> x0, local copies, waits for them, and re-layouts: 14.6 us -> none  [split_heads(): return matrix.reshape(groups, -1, matrix.shape[1] // HEAD_DIM, HEAD_DIM)]
  transfers between devices with their start and end apart: 16 -> 0, of which waited for: 12 -> 0; matrix products, arithmetic and copies ran while one was open for 8% -> 0% of each run, Pallas kernels for 0% -> 0%
where the time goes in v1:
time: 156 us
  Pallas kernels  124 us (79%)
  local copies, waits for them, and re-layouts  31.2 us (20%)
    pallas_call x1, Pallas kernels, on_device(): pl.pallas_call(body, out_shape=[jax.ShapeDtypeStruct(*s) for s in shapes]...  124 us
    unnamed x37, local copies, waits for them, and re-layouts  28.4 us

profile of v1, /device:TPU:0, one launch (start us, length us, event | category | flops | bytes accessed | tf_op | source)
XLA Modules:
  0.0 155.6 jit_solution(3742449912224918365)
XLA Ops:
  0.7 1.9 %copy.41.refs_12_ = bf16[768,192]{1,0:T(8,128)(2,1)} copy(bf16[768,192]{0,1:T(8,128)(2,1)} %param.34) | data formatting | bytes 589824 | tf_op args[12]
  2.5 1.9 %copy.42.refs_13_ = bf16[768,192]{1,0:T(8,128)(2,1)} copy(bf16[768,192]{0,1:T(8,128)(2,1)} %param.35) | data formatting | bytes 589824 | tf_op args[13]
  4.4 1.9 %copy.43.refs_14_ = bf16[768,192]{1,0:T(8,128)(2,1)} copy(bf16[768,192]{0,1:T(8,128)(2,1)} %param.36) | data formatting | bytes 589824 | tf_op args[14]
  6.3 1.9 %copy.44.refs_16_ = bf16[768,192]{1,0:T(8,128)(2,1)} copy(bf16[768,192]{0,1:T(8,128)(2,1)} %param.38) | data formatting | bytes 589824 | tf_op args[16]
  8.2 1.9 %copy.45.refs_17_ = bf16[768,192]{1,0:T(8,128)(2,1)} copy(bf16[768,192]{0,1:T(8,128)(2,1)} %param.39) | data formatting | bytes 589824 | tf_op args[17]
  10.1 1.9 %copy.46.refs_18_ = bf16[768,192]{1,0:T(8,128)(2,1)} copy(bf16[768,192]{0,1:T(8,128)(2,1)} %param.40) | data formatting | bytes 589824 | tf_op args[18]
  11.9 123.7 %layer.1 = (bf16[448,768]{1,0:T(8,128)(2,1)}, bf16[448,768]{1,0:T(8,128)(2,1)}, bf16[3584,768]{1,0:T(8,128)(2,1)}, f32[96,192]{1,0:T(8,128)}, f32[96,192]{1,0:T(...) custom-call(bf16[448,768]{1,0:T(8,128)(2,1)} %refs_0_.1, ...), custom_call_target="tpu_custom_call" | custom-call | tf_op jit(solution)/shard_map/layer/pallas_call | solution.py:828
  135.6 1.0 fusion.6
  136.6 0.6 fusion.4
  137.2 0.6 fusion.2
  137.8 0.6 fusion
  138.3 1.9 %copy.47 = f32[768,96]{0,1:T(8,128)} copy(f32[768,96]{1,0:T(8,128)} %get-tuple-element.59) | data formatting | bytes 589824
  140.2 2.0 %copy.60 = bf16[448,768]{1,0:T(8,128)(2,1)} copy(bf16[448,768]{1,0:T(8,128)(2,1)} %get-tuple-element.97) | data formatting | bytes 1376256
  142.2 2.0 %copy.61 = bf16[448,768]{1,0:T(8,128)(2,1)} copy(bf16[448,768]{1,0:T(8,128)(2,1)} %get-tuple-element.98) | data formatting | bytes 1376256
  144.3 5.4 %copy.62 = bf16[3584,768]{1,0:T(8,128)(2,1)} copy(bf16[3584,768]{1,0:T(8,128)(2,1)} %get-tuple-element.99) | data formatting | bytes 11010048
  149.7 0.6 copy.63
  150.3 0.6 copy.64
  151.0 0.6 copy.65
  151.6 0.6 copy.66
  152.3 0.6 copy.67
  152.9 0.6 copy.68
  153.6 0.6 copy.69
  154.2 0.6 copy.70
  154.9 0.7 copy.71
  (18 shorter events, 0.0 us)
Async XLA Ops:
  144.2 5.5 %copy-start.8 = (f32[96,192]{1,0:T(8,128)S(1)}, f32[96,192]{1,0:T(8,128)}, u32[]{:S(2)}) copy-start(f32[96,192]{1,0:T(8,128)} %get-tuple-element.100) | copy-start | bytes 221188
  144.2 6.2 %copy-start.7 = (f32[96,192]{1,0:T(8,128)S(1)}, f32[96,192]{1,0:T(8,128)}, u32[]{:S(2)}) copy-start(f32[96,192]{1,0:T(8,128)} %get-tuple-element.101) | copy-start | bytes 221188
  144.2 6.8 %copy-start.6 = (f32[96,192]{1,0:T(8,128)S(1)}, f32[96,192]{1,0:T(8,128)}, u32[]{:S(2)}) copy-start(f32[96,192]{1,0:T(8,128)} %get-tuple-element.102) | copy-start | bytes 221188
  144.2 7.4 %copy-start.5 = (f32[192,96]{1,0:T(8,128)S(1)}, f32[192,96]{1,0:T(8,128)}, u32[]{:S(2)}) copy-start(f32[192,96]{1,0:T(8,128)} %get-tuple-element.103) | copy-start | bytes 221188
  144.2 8.1 %copy-start.4 = (f32[96,192]{1,0:T(8,128)S(1)}, f32[96,192]{1,0:T(8,128)}, u32[]{:S(2)}) copy-start(f32[96,192]{1,0:T(8,128)} %get-tuple-element.104) | copy-start | bytes 221188
  144.2 8.7 %copy-start.3 = (f32[96,192]{1,0:T(8,128)S(1)}, f32[96,192]{1,0:T(8,128)}, u32[]{:S(2)}) copy-start(f32[96,192]{1,0:T(8,128)} %get-tuple-element.105) | copy-start | bytes 221188
  144.2 9.3 %copy-start.2 = (f32[96,192]{1,0:T(8,128)S(1)}, f32[96,192]{1,0:T(8,128)}, u32[]{:S(2)}) copy-start(f32[96,192]{1,0:T(8,128)} %get-tuple-element.106) | copy-start | bytes 221188
  144.2 10.0 %copy-start.1 = (f32[192,96]{1,0:T(8,128)S(1)}, f32[192,96]{1,0:T(8,128)}, u32[]{:S(2)}) copy-start(f32[192,96]{1,0:T(8,128)} %get-tuple-element.107) | copy-start | bytes 221188
  144.2 10.6 %copy-start = (f32[96,768]{1,0:T(8,128)S(1)}, f32[96,768]{1,0:T(8,128)}, u32[]{:S(2)}) copy-start(f32[96,768]{1,0:T(8,128)} %get-tuple-element.108) | copy-start | bytes 884740

commit v2 on v1

--- a/solution.py
+++ b/solution.py
@@ -17,6 +17,7 @@
 UNIT = 384
 ROWS = 32
 N_SEMS = 160
+VMEM_BYTES = 52 * 2**20
 
 
 def nn(a, b):
@@ -136,9 +137,7 @@
     vmem("xin", (T, D))
     vmem("cot", (T, D))
     vmem("mem", (MO, D))
-    for n in ("raw_sq", "raw_sk", "raw_sv", "raw_cq", "raw_ck", "raw_cv"):
-        vmem(n, (D, C))
-    vmem("wqkv", (D, 3 * C))
+    vmem("wqkv", (3 * C, D))
     vmem("so", (C, D))
     for n in ("cq", "ck", "cv", "co"):
         vmem(n, (H, D))
@@ -160,7 +159,7 @@
     vmem("c2", (RO, D))
     for n in ("q2", "o2", "do2", "dq2"):
         vmem(n, (RO, H))
-    for n in ("k2", "v2", "dk2", "dv2"):
+    for n in ("k2", "v2"):
         vmem(n, (MO, H))
     for n in ("p2", "ds2"):
         vmem(n, (d.GO * d.NB, 4 * d.S, K))
@@ -169,9 +168,6 @@
     vmem("act", (T, F))
     vmem("du", (T, F))
     vmem("dact", (T, F), F32)
-    vmem("mg", (d.GO, K, D))
-    vmem("lo", (RO, D))
-    vmem("sg", (RO, D))
     for n in ("cs1", "cs2", "cr1", "cr2"):
         vmem(n, (d.nch, d.rp, UNIT))
     for u in UNITS:
@@ -213,7 +209,7 @@
         return {"dp": dp + (1 << b) * (1 - 2 * bit_of(b))}
 
     state = {"r": 0, "l": 0}
-    sends, locals_ = [], []
+    sends = []
 
     def remote(src, dst, device, index=None):
         if index is None:
@@ -243,14 +239,14 @@
 
     ld = {}
     mp_rows = pl.ds(pl.multiple_of(mp * d.C, 16), d.C)
-    ld["ck"] = load(r.cross_key, r.raw_ck)
-    ld["cv"] = load(r.cross_value, r.raw_cv)
-    ld["cq"] = load(r.cross_query, r.raw_cq)
+    ld["ck"] = load(r.cross_key, r.ck.at[mp_rows])
+    ld["cv"] = load(r.cross_value, r.cv.at[mp_rows])
+    ld["cq"] = load(r.cross_query, r.cq.at[mp_rows])
     ld["co"] = load(r.cross_out, r.co.at[mp_rows])
     ld["xin"] = load(r.suffix, r.xin)
-    ld["sq"] = load(r.self_query, r.raw_sq)
-    ld["sk"] = load(r.self_key, r.raw_sk)
-    ld["sv"] = load(r.self_value, r.raw_sv)
+    ld["sq"] = load(r.self_query, r.wqkv.at[pl.ds(0, d.C)])
+    ld["sk"] = load(r.self_key, r.wqkv.at[pl.ds(d.C, d.C)])
+    ld["sv"] = load(r.self_value, r.wqkv.at[pl.ds(2 * d.C, d.C)])
     ld["so"] = load(r.self_out, r.so)
     ld["cot"] = load(r.cotangent, r.cot)
     ld["dn"] = load(r.mlp_down, r.dn)
@@ -266,7 +262,6 @@
     PC = d.C // 2
     piece = lax.rem(dp, 2)
     full = {"ck": r.ck, "cv": r.cv, "cq": r.cq, "co": r.co}
-    raw = {"ck": r.raw_ck, "cv": r.raw_cv, "cq": r.raw_cq}
     xm = lax.rem(mp + 2, 4)
     gat = {}
 
@@ -276,8 +271,6 @@
     def gather_start(w):
         ref = full[w]
         ld[w].wait()
-        if w in raw:
-            ref[mp_rows, :] = raw[w][...].T
         mine = part(ref, mp, piece)
         gat[w, "x"] = send(mine, mine, xmate)
         gat[w, "s"] = send(ref.at[mp_rows], ref.at[mp_rows], sib)
@@ -359,7 +352,7 @@
 
     def fin_dn(lane):
         def f(v):
-            r.g_dn[lane : lane + UNIT, :] = v.T
+            r.g_dn[:, lane : lane + UNIT] = v
 
         return f
 
@@ -445,10 +438,9 @@
         return c
 
     row_loop(d.T, norm_one)
-    for k, n in enumerate(("sq", "sk", "sv")):
+    for n in ("sq", "sk", "sv"):
         ld[n].wait()
-        r.wqkv[:, k * d.C : (k + 1) * d.C] = getattr(r, "raw_" + n)[...]
-    qkv = nn(r.a1[...], r.wqkv[...])
+    qkv = nt(r.a1[...], r.wqkv[...])
     r.q1[: d.T, :] = (qkv[:, : d.C] * factor).astype(BF)
     r.k1[: d.T, :] = qkv[:, d.C : 2 * d.C].astype(BF)
     r.v1[: d.T, :] = qkv[:, 2 * d.C :].astype(BF)
@@ -645,7 +637,7 @@
         r.dqkv[b, : d.C] = dq.astype(BF)
         r.dqkv[b, d.C : 2 * d.C] = dk.astype(BF)
         r.dqkv[b, 2 * d.C :] = dv.astype(BF)
-    x6 = reduce_rows(6, lambda s: nt(r.dqkv[s, :], r.wqkv[...]))
+    x6 = reduce_rows(6, lambda s: nn(r.dqkv[s, :], r.wqkv[...]))
     rows = slice(0, d.T)
     units["s1"].store(tn(r.a1[...], r.dqkv[rows, : 2 * d.C]), 0)
     units["s1"].go()
@@ -660,8 +652,8 @@
         for b in range(d.NB):
             lanes = slice(256 * b, 256 * b + 256)
             j = g * d.NB + b
-            r.dk2[ks, lanes] = tn(r.ds2[j], spread(r.q2[qs, lanes], hb2)).astype(BF)
-            r.dv2[ks, lanes] = tn(r.p2[j], spread(r.do2[qs, lanes], hb2)).astype(BF)
+            r.k2[ks, lanes] = tn(r.ds2[j], spread(r.q2[qs, lanes], hb2)).astype(BF)
+            r.v2[ks, lanes] = tn(r.p2[j], spread(r.do2[qs, lanes], hb2)).astype(BF)
         return c
 
     lax.fori_loop(0, d.GO, cross_keys, 0)
@@ -683,7 +675,7 @@
     split_columns(units["c1"], away1, 0, tn(r.a2[...], r.dq2[:, pair]))
     split_columns(units["c1"], away1, d.C, tn(r.c2[...], r.o2[:, pair]))
     cc1 = send(r.cs1, r.cr1, sib)
-    split_columns(units["c2"], away2, 0, tn(r.mem[...], r.dk2[:, pair]))
+    split_columns(units["c2"], away2, 0, tn(r.mem[...], r.k2[:, pair]))
 
     def merge(unit, cp, got):
         cp.wait_recv()
@@ -692,7 +684,7 @@
         unit.go()
 
     merge(units["c1"], cc1, r.cr1)
-    split_columns(units["c2"], away2, d.C, tn(r.mem[...], r.dv2[:, pair]))
+    split_columns(units["c2"], away2, d.C, tn(r.mem[...], r.v2[:, pair]))
     cc2 = send(r.cs2, r.cr2, sib)
     steps("u1", "u2")
 
@@ -700,12 +692,11 @@
 
     def finish_out(i, c):
         s = pl.ds(i, ROWS)
-        r.lo[s, :] = (r.h2[s, :] + total(3, s)).astype(BF)
+        r.layer_out[pl.ds(pl.multiple_of(own + i, 16), ROWS), :] = (r.h2[s, :] + total(3, s)).astype(BF)
         return c
 
     row_loop(d.RO, finish_out)
-    tail = [send(r.lo, r.layer_out.at[own_rows], sib)]
-    locals_.append(load(r.lo, r.layer_out.at[own_rows]))
+    tail = [send(r.layer_out.at[own_rows], r.layer_out.at[own_rows], sib)]
     merge(units["c2"], cc2, r.cr2)
 
     x6.wait_recv()
@@ -716,12 +707,13 @@
         s = pl.ds(i, ROWS)
         e = total(6, s)
         z, inv = normalize(r.xin[pl.ds(pl.multiple_of(own + i, 16), ROWS), :].astype(F32))
-        r.sg[s, :] = (r.dh[s, :] + norm_back(z, inv, gain, e)).astype(BF)
+        r.suffix_grad[pl.ds(pl.multiple_of(own + i, 16), ROWS), :] = (
+            r.dh[s, :] + norm_back(z, inv, gain, e)
+        ).astype(BF)
         return gg + fold8(e * z), gs + fold8(e)
 
     gain_self_grad, shift_self_grad = row_loop(d.RO, back_one, (zero8, zero8))
-    tail.append(send(r.sg, r.suffix_grad.at[own_rows], sib))
-    locals_.append(load(r.sg, r.suffix_grad.at[own_rows]))
+    tail.append(send(r.suffix_grad.at[own_rows], r.suffix_grad.at[own_rows], sib))
     for k, v in enumerate(
         (
             gain_self_grad,
@@ -744,23 +736,18 @@
             return send(r.nst.at[k + 1], r.nrc.at[k + 1], devices[k + 1])
         return None
 
-    base_r, base_l = state["r"], state["l"]
+    base_r = state["r"]
     state["r"] += d.GO
-    state["l"] += d.GO
-
-    def memory_copies(g):
+
+    def memory_copy(g):
         rows = pl.ds(pl.multiple_of(core * d.MO + g * d.K, 16), d.K)
-        there = remote(r.mg.at[g], r.memory_grad.at[rows], sib, base_r + g)
-        here = pltpu.make_async_copy(r.mg.at[g], r.memory_grad.at[rows], r.ls.at[base_l + g])
-        return there, here
+        return remote(r.memory_grad.at[rows], r.memory_grad.at[rows], sib, base_r + g)
 
     def memory_group(g, c):
         ks = pl.ds(pl.multiple_of(g * d.K, d.K), d.K)
-        value = nn(r.dk2[ks, :], r.ck[...]) + nn(r.dv2[ks, :], r.cv[...])
-        r.mg[g] = value.astype(BF)
-        there, here = memory_copies(g)
-        there.start()
-        here.start()
+        value = nn(r.k2[ks, :], r.ck[...]) + nn(r.v2[ks, :], r.cv[...])
+        r.memory_grad[pl.ds(pl.multiple_of(core * d.MO + g * d.K, 16), d.K), :] = value.astype(BF)
+        memory_copy(g).start()
         return c
 
     lax.fori_loop(0, d.GO, memory_group, 0)
@@ -781,12 +768,7 @@
             if units[u].stage < d.bits:
                 units[u].step()
     for g in range(d.GO):
-        there, here = memory_copies(g)
-        there.wait_recv()
-        there.wait_send()
-        here.wait()
-    for cp in locals_:
-        cp.wait()
+        memory_copy(g).wait()
     for cp in tail:
         cp.wait_recv()
     for cp in sends:
@@ -816,7 +798,7 @@
             (col, F32),
             (turned, F32),
             ((d.rp, d.F), F32),
-            ((d.F, d.rp), F32),
+            ((d.rp, d.F), F32),
             ((8, d.D), F32),
         ]
         hbm, vmem = pl.BlockSpec(memory_space=pl.ANY), pl.BlockSpec(memory_space=pltpu.VMEM)
@@ -827,23 +809,49 @@
 
         outs = pl.pallas_call(
             body,
-            out_shape=[jax.ShapeDtypeStruct(*s) for s in shapes],
+            out_shape=[pltpu.VMEM(*s) for s in shapes],
             in_specs=[hbm] * 3 + [smem] * 3 + [vmem] * 6 + [hbm] * 10,
-            out_specs=[hbm] * 3 + [vmem] * 11,
+            out_specs=[vmem] * 14,
             scratch_shapes=list(scr.values()),
             compiler_params=pltpu.CompilerParams(
-                collective_id=0, has_side_effects=True, vmem_limit_bytes=67043328
+                collective_id=0, has_side_effects=True, vmem_limit_bytes=VMEM_BYTES
             ),
             name="layer",
-        )(*args)
-        big, grads, norms = outs[:3], list(outs[3:13]), outs[13]
+        )(*(a.T if k in (12, 13, 14, 16, 17, 18) else a for k, a in enumerate(args)))
+        outs = [pltpu.with_memory_space_constraint(o, pltpu.VMEM) for o in outs]
+        rows = d.D // n_dp
+
+        def write(*refs):
+            ins, norms, dst, vectors, sem = refs[:13], refs[13], refs[14:27], refs[27:33], refs[33]
+            copies = [
+                pltpu.make_async_copy(a, b, sem.at[k]) for k, (a, b) in enumerate(zip(ins, dst))
+            ]
+            for cp in copies:
+                cp.start()
+            shift = lax.rem(d.D - lax.axis_index("dp") * rows, d.D)
+            mine = pltpu.roll(norms[...], shift, 1)
+            for k, v in enumerate(vectors):
+                v[...] = mine[k, :rows]
+            for cp in copies:
+                cp.wait()
+
+        final = pl.pallas_call(
+            write,
+            out_shape=[jax.ShapeDtypeStruct(*s) for s in shapes[:13]]
+            + [jax.ShapeDtypeStruct((rows,), F32)] * 6,
+            in_specs=[vmem] * 14,
+            out_specs=[hbm] * 13 + [vmem] * 6,
+            scratch_shapes=[pltpu.SemaphoreType.DMA((13,))],
+            compiler_params=pltpu.CompilerParams(vmem_limit_bytes=2**20),
+            name="write",
+        )(*outs)
+        big, grads, vectors = final[:3], list(final[3:13]), final[13:]
         dp = lax.axis_index("dp")
-        rows = d.D // n_dp
         if d.low:
             start = lax.rem(dp, 1 << d.low) * rows
-            for k, turn in enumerate((0, 0, 0, 1, 0, 0, 0, 1, 0, 1)):
+            for k, turn in enumerate((0, 0, 0, 1, 0, 0, 0, 1, 0, 0)):
                 grads[k] = lax.dynamic_slice_in_dim(grads[k], start, rows, axis=turn)
-        vectors = [lax.dynamic_slice_in_dim(norms[k], dp * rows, rows, axis=0) for k in range(6)]
+        grads[9] = grads[9].T
         return (*big, *grads, *vectors)
 
     row, col, turn = P("dp", None), P("dp", "mp"), P("mp", "dp")

time: 156 us -> 127 us (0.81)
  local copies, waits for them, and re-layouts: 31.2 us -> 0 us
  Pallas kernels: 124 us -> 126 us
    unnamed x37 -> x0, local copies, waits for them, and re-layouts: 28.4 us -> none
    pallas_call x1 -> x2, Pallas kernels: 124 us -> 126 us  [the longest x1 122 us: on_device(): pl.pallas_call(body, out_shape=[pltpu.VMEM(*s) for s in shapes], in_specs...]
    dynamic_slice x3 -> x0, local copies, waits for them, and re-layouts: 1.77 us -> none  [on_device(): lax.dynamic_slice_in_dim(norms[k], dp * rows, rows, axis=0)]
where the time goes in v2:
time: 127 us
  Pallas kernels  126 us (99%)
    pallas_call x1, Pallas kernels, on_device(): pl.pallas_call(body, out_shape=[pltpu.VMEM(*s) for s in shapes], in_specs...  122 us
    pallas_call x1, Pallas kernels, on_device(): pl.pallas_call(write, out_shape=[jax.ShapeDtypeStruct(*s) for s in shapes...  4.01 us

profile of v2, /device:TPU:0, one launch (start us, length us, event | category | flops | bytes accessed | tf_op | source)
XLA Modules:
  0.0 127.1 jit_solution(15717712775635200117)
XLA Ops:
  0.7 122.3 %layer.1 = (bf16[448,768]{1,0:T(8,128)(2,1)S(1)}, bf16[448,768]{1,0:T(8,128)(2,1)S(1)}, bf16[3584,768]{1,0:T(8,128)(2,1)S(1)}, f32[96,192]{1,0:T(8,128)S(1)}, f3...) custom-call(bf16[448,768]{1,0:T(8,128)(2,1)} %refs_0_.1, ...), custom_call_target="tpu_custom_call" | custom-call | tf_op jit(solution)/shard_map/layer/pallas_call | solution.py:810
  122.9 4.0 %write.1 = (bf16[448,768]{1,0:T(8,128)(2,1)}, bf16[448,768]{1,0:T(8,128)(2,1)}, bf16[3584,768]{1,0:T(8,128)(2,1)}, f32[96,192]{1,0:T(8,128)}, f32[96,192]{1,0:T(...) custom-call(bf16[448,768]{1,0:T(8,128)(2,1)S(1)} %get-tuple-element., ...), custom_call_target="tpu_custom_call" | custom-call | tf_op jit(solution)/shard_map/write/pallas_call | solution.py:838

commit v3 on v2

--- a/solution.py
+++ b/solution.py
@@ -15,9 +15,9 @@
 EPSILON = 1e-06
 NEG_FILL = -1e30
 UNIT = 384
-ROWS = 32
+ROWS = 112
 N_SEMS = 160
-VMEM_BYTES = 52 * 2**20
+VMEM_BYTES = 54 * 2**20
 
 
 def nn(a, b):
@@ -74,7 +74,7 @@
         self.BLK = pl.cdiv(self.T, 128)
         self.TP = self.BLK * 128
         self.bits = n_dp.bit_length() - 1
-        assert 1 << self.bits == n_dp
+        assert 1 << self.bits == n_dp and n_dp >= 4
         halvings = 0
         while halvings < self.bits and (self.D >> (halvings + 1)) % 16 == 0:
             halvings += 1
@@ -208,6 +208,8 @@
     def mate(b):
         return {"dp": dp + (1 << b) * (1 - 2 * bit_of(b))}
 
+    corner = {"dp": dp + 3 - 2 * bit_of(0) - 4 * bit_of(1)}
+
     state = {"r": 0, "l": 0}
     sends = []
 
@@ -254,15 +256,16 @@
     ld["up"] = load(r.mlp_up, r.up)
 
     barrier = pltpu.get_barrier_semaphore()
-    mates = [sib, xmate] + [mate(b) for b in range(d.bits)]
+    mates = [sib, xmate, corner] + [mate(b) for b in range(d.bits)]
     for device in mates:
         pl.semaphore_signal(barrier, inc=1, device_id=device, device_id_type=MESH)
     pl.semaphore_wait(barrier, len(mates))
 
-    PC = d.C // 2
-    piece = lax.rem(dp, 2)
+    PC = d.C // 4
+    piece = lax.rem(dp, 4)
     full = {"ck": r.ck, "cv": r.cv, "cq": r.cq, "co": r.co}
     xm = lax.rem(mp + 2, 4)
+    xm_rows = pl.ds(pl.multiple_of(xm * d.C, 16), d.C)
     gat = {}
 
     def part(ref, owner, which):
@@ -278,24 +281,27 @@
     def gather_x(w):
         gat[w, "x"].wait_recv()
         got = part(full[w], xm, piece)
-        gat[w, "y"] = send(got, got, mate(0))
-        gat[w, "sx"] = send(got, got, sib)
+        for k, device in enumerate((mate(0), mate(1), corner)):
+            gat[w, k] = send(got, got, device)
 
     def gather_y(w):
-        gat[w, "y"].wait_recv()
-        got = part(full[w], xm, 1 - piece)
-        gat[w, "sy"] = send(got, got, sib)
+        for k in range(3):
+            gat[w, k].wait_recv()
+        gat[w, "f"] = send(full[w].at[xm_rows], full[w].at[xm_rows], sib)
 
     def gather_done(w):
-        for k in ("s", "sx", "sy"):
-            gat[w, k].wait_recv()
+        gat[w, "s"].wait_recv()
+        gat[w, "f"].wait_recv()
 
     for w in ("ck", "cv", "cq", "co"):
         gather_start(w)
 
     class Unit:
-        def __init__(self, name, finish):
+        def __init__(self, name, finish, swap=False):
             self.name, self.finish, self.stage = name, finish, 0
+            self.order = list(range(d.halvings))
+            if swap:
+                self.order[:2] = 1, 0
             self.acc = getattr(r, f"g_{name}_acc")
             self.base = 0
             self.cp = None
@@ -303,14 +309,14 @@
         def store(self, value, lane):
             width = value.shape[1]
             for j in range(d.nch):
-                p = sum(((j >> k) & 1) * (d.nch >> (k + 1)) for k in range(d.halvings))
+                p = sum(((j >> b) & 1) * (d.nch >> (k + 1)) for k, b in enumerate(self.order))
                 self.acc[p, :, lane : lane + width] = value[j * d.rp : (j + 1) * d.rp].astype(BF)
 
         def go(self):
             k = self.stage
             if k < d.halvings:
                 half = d.nch >> (k + 1)
-                b = d.low + k
+                b = d.low + self.order[k]
                 dst = getattr(r, f"g_{self.name}_r{k}")
                 src = self.acc.at[pl.ds(self.base + (1 - bit_of(b)) * half, half)]
                 self.cp = send(src, dst, mate(b))
@@ -326,7 +332,7 @@
             if k < d.halvings:
                 half = d.nch >> (k + 1)
                 got = getattr(r, f"g_{self.name}_r{k}")
-                base = self.base + bit_of(d.low + k) * half
+                base = self.base + bit_of(d.low + self.order[k]) * half
                 self.base = base
                 if k < d.halvings - 1:
                     for j in range(half):
@@ -371,11 +377,11 @@
 
     units = {
         "d1": Unit("d1", fin_dn(0)),
-        "d2": Unit("d2", fin_dn(UNIT)),
+        "d2": Unit("d2", fin_dn(UNIT), True),
         "u1": Unit("u1", fin_up(0)),
         "u2": Unit("u2", fin_up(UNIT)),
         "s1": Unit("s1", fin_pair(r.g_sq, r.g_sk, False)),
-        "s2": Unit("s2", fin_pair(r.g_sv, r.g_so, True)),
+        "s2": Unit("s2", fin_pair(r.g_sv, r.g_so, True), True),
         "c1": Unit("c1", fin_pair(r.g_cq, r.g_co, True)),
         "c2": Unit("c2", fin_pair(r.g_ck, r.g_cv, False)),
     }
@@ -385,10 +391,12 @@
             if units[u].stage < d.bits:
                 units[u].step()
 
-    def reduce_rows(k, partial):
-        s, got, xs, xr = (getattr(r, f"{n}{k}") for n in ("s", "r", "xs", "xr"))
-        s[...] = partial(other_rows).astype(BF)
-        cp = send(s, got, sib)
+    def reduce_begin(k, partial):
+        getattr(r, f"s{k}")[...] = partial(other_rows).astype(BF)
+        return send(getattr(r, f"s{k}"), getattr(r, f"r{k}"), sib)
+
+    def reduce_end(k, partial, cp):
+        got, xs, xr = (getattr(r, f"{n}{k}") for n in ("r", "xs", "xr"))
         value = partial(own_rows)
         cp.wait_recv()
         xs[...] = (value + got[...].astype(F32)).astype(BF)
@@ -468,18 +476,21 @@
         r.o1[b, :] = gatherh(nn(p, r.v1[b, :]), hf1).astype(BF)
     gather_x("cv")
     ld["so"].wait()
-    x1 = reduce_rows(1, lambda s: nn(r.o1[s, :], r.so[...]))
-    gather_x("cq")
-    gather_y("ck")
-
+
+    def out_one(rows):
+        return nn(r.o1[rows, :], r.so[...])
+
+    x1 = reduce_begin(1, out_one)
     ld["cot"].wait()
     ld["dn"].wait()
     r.dact[...] = nt(r.cot[...], r.dn[...])
-    gather_y("cv")
+    x1 = reduce_end(1, out_one, x1)
+
+    gather_x("cq")
     gather_x("co")
+    gather_y("ck")
     ld["mem"].wait()
-    gather_done("ck")
-    big = d.MO // 4
+    big = d.MO // 2
 
     def project(w, dst):
         def body(i, c):
@@ -487,13 +498,14 @@
             dst[s, :] = nt(r.mem[s, :], w[...]).astype(BF)
             return c
 
-        lax.fori_loop(0, 4, body, 0)
-
+        lax.fori_loop(0, 2, body, 0)
+
+    gather_done("ck")
     project(r.ck, r.k2)
-    gather_y("cq")
+    gather_y("cv")
     gather_done("cv")
     project(r.cv, r.v2)
-    gather_y("co")
+    gather_y("cq")
 
     x1.wait_recv()
     gain, shift = vec(r.gain_cross), vec(r.shift_cross)
@@ -511,20 +523,29 @@
     r.q2[...] = (nt(r.a2[...], r.cq[...]) * factor).astype(BF)
     slot = lax.broadcasted_iota(jnp.int32, (4 * d.S, d.K), 1)
 
+    blocks = [slice(256 * b, 256 * b + 256) for b in range(d.NB)]
+
     def cross_forward(g, c):
         n = core * d.GO + g
         live = r.kind[n] * PATCHES + r.prefix[n]
         qs = pl.ds(pl.multiple_of(g * d.S, d.S), d.S)
         ks = pl.ds(pl.multiple_of(g * d.K, d.K), d.K)
-        for b in range(d.NB):
-            lanes = slice(256 * b, 256 * b + 256)
-            scores = nt(spread(r.q2[qs, lanes], hb2), r.k2[ks, lanes])
-            p = softmax(jnp.where(slot < live, scores, NEG_FILL)).astype(BF)
-            r.p2[g * d.NB + b] = p
-            r.o2[qs, lanes] = gatherh(nn(p, r.v2[ks, lanes]), hf2).astype(BF)
+        v = [r.v2[ks, b] for b in blocks]
+        s = [nt(spread(r.q2[qs, b], hb2), r.k2[ks, b]) for b in blocks]
+        s = [jnp.where(slot < live, x, NEG_FILL) for x in s]
+        top = [jnp.max(x, axis=-1, keepdims=True) for x in s]
+        p = [jnp.exp(x - t) for x, t in zip(s, top)]
+        scale = [1.0 / jnp.sum(x, axis=-1, keepdims=True) for x in p]
+        p = [(x * t).astype(BF) for x, t in zip(p, scale)]
+        o = [nn(x, y) for x, y in zip(p, v)]
+        o = [gatherh(x, hf2).astype(BF) for x in o]
+        for k, b in enumerate(blocks):
+            r.p2[g * d.NB + k] = p[k]
+            r.o2[qs, b] = o[k]
         return c
 
     lax.fori_loop(0, d.GO, cross_forward, 0)
+    gather_y("co")
     gather_done("co")
     r.tmp[...] = nn(r.o2[...], r.co[...])
     gain, shift = vec(r.gain_mlp), vec(r.shift_mlp)
@@ -561,14 +582,23 @@
     hidden(own)
     a3.wait_recv()
     hidden(other)
-    x4 = reduce_rows(4, lambda s: nt(r.du[s, :], r.up[...]))
+
+    def back_four(rows):
+        return nt(r.du[rows, :], r.up[...])
+
+    def out_three(rows):
+        return nn(r.act[rows, :], r.dn[...])
+
+    x4 = reduce_begin(4, back_four)
     for u, lane in (("d1", 0), ("d2", UNIT)):
         units[u].store(tn(r.cot[...], r.act[:, lane : lane + UNIT]), 0)
         units[u].go()
+    x4 = reduce_end(4, back_four, x4)
+    x3 = reduce_begin(3, out_three)
     for u, lane in (("u1", 0), ("u2", UNIT)):
         units[u].store(tn(r.a3[...], r.du[:, lane : lane + UNIT]), 0)
         units[u].go()
-    x3 = reduce_rows(3, lambda s: nn(r.act[s, :], r.dn[...]))
+    x3 = reduce_end(3, out_three, x3)
 
     x4.wait_recv()
     gain = vec(r.gain_mlp)
@@ -592,18 +622,23 @@
     def cross_backward(g, c):
         qs = pl.ds(pl.multiple_of(g * d.S, d.S), d.S)
         ks = pl.ds(pl.multiple_of(g * d.K, d.K), d.K)
-        for b in range(d.NB):
-            lanes = slice(256 * b, 256 * b + 256)
-            dp_ = nt(spread(r.do2[qs, lanes], hb2), r.v2[ks, lanes])
-            p = r.p2[g * d.NB + b].astype(F32)
-            t = p * dp_
-            ds = (t - p * jnp.sum(t, axis=-1, keepdims=True)).astype(BF)
-            r.ds2[g * d.NB + b] = ds
-            r.dq2[qs, lanes] = (gatherh(nn(ds, r.k2[ks, lanes]), hf2) * factor).astype(BF)
+        k2 = [r.k2[ks, b] for b in blocks]
+        p = [r.p2[g * d.NB + k].astype(F32) for k in range(d.NB)]
+        t = [nt(spread(r.do2[qs, b], hb2), r.v2[ks, b]) for b in blocks]
+        t = [x * y for x, y in zip(p, t)]
+        centre = [jnp.sum(x, axis=-1, keepdims=True) for x in t]
+        ds = [(x - y * m).astype(BF) for x, y, m in zip(t, p, centre)]
+        dq = [nn(x, y) for x, y in zip(ds, k2)]
+        dq = [(gatherh(x, hf2) * factor).astype(BF) for x in dq]
+        for k, b in enumerate(blocks):
+            r.ds2[g * d.NB + k] = ds[k]
+            r.dq2[qs, b] = dq[k]
         return c
 
+    steps("d1", "d2")
     lax.fori_loop(0, d.GO, cross_backward, 0)
     r.tmp[...] = nn(r.dq2[...], r.cq[...])
+    steps("u1")
     gain = vec(r.gain_cross)
 
     def back_two(i, c):
@@ -618,8 +653,31 @@
 
     gain_cross_grad, shift_cross_grad = row_loop(d.RO, back_two, (zero8, zero8))
     c1 = send(r.c1.at[own_rows], r.c1.at[own_rows], sib)
-    steps("d1", "d2")
-
+    pair = pl.ds(pl.multiple_of((mp // 2) * 2 * d.C, 128), 2 * d.C)
+
+    def split_columns(unit, away, lane, value):
+        left, right = value[:, : d.C], value[:, d.C :]
+        first = core == 0
+        unit.store(jnp.where(first, left, right), lane)
+        away.store(jnp.where(first, right, left), lane)
+
+    class Away:
+        def __init__(self, ref, order):
+            self.acc, self.order = ref, order
+
+        store = Unit.store
+
+    away1 = Away(r.cs1, units["c1"].order)
+    away2 = Away(r.cs2, units["c2"].order)
+    def merge(unit, cp, got):
+        cp.wait_recv()
+        for j in range(d.nch):
+            unit.acc[j] = (unit.acc[j].astype(F32) + got[j].astype(F32)).astype(BF)
+        unit.go()
+
+    split_columns(units["c1"], away1, 0, tn(r.a2[...], r.dq2[:, pair]))
+    split_columns(units["c1"], away1, d.C, tn(r.c2[...], r.o2[:, pair]))
+    cc1 = send(r.cs1, r.cr1, sib)
     r.do1[own_rows, :] = nt(r.c1[own_rows, :], r.so[...]).astype(BF)
     c1.wait_recv()
     r.do1[other_rows, :] = nt(r.c1[other_rows, :], r.so[...]).astype(BF)
@@ -637,57 +695,38 @@
         r.dqkv[b, : d.C] = dq.astype(BF)
         r.dqkv[b, d.C : 2 * d.C] = dk.astype(BF)
         r.dqkv[b, 2 * d.C :] = dv.astype(BF)
-    x6 = reduce_rows(6, lambda s: nn(r.dqkv[s, :], r.wqkv[...]))
+    steps("d1", "d2")
+
+    def back_six(rows):
+        return nn(r.dqkv[rows, :], r.wqkv[...])
+
     rows = slice(0, d.T)
+    x6 = reduce_begin(6, back_six)
     units["s1"].store(tn(r.a1[...], r.dqkv[rows, : 2 * d.C]), 0)
     units["s1"].go()
+    x6 = reduce_end(6, back_six, x6)
     units["s2"].store(tn(r.a1[...], r.dqkv[rows, 2 * d.C :]), 0)
     units["s2"].store(tn(r.c1[...], r.o1[rows, :]), d.C)
     units["s2"].go()
-    steps("u1", "u2", "d1", "d2")
+    merge(units["c1"], cc1, r.cr1)
+    steps("u2", "u1")
 
     def cross_keys(g, c):
         qs = pl.ds(pl.multiple_of(g * d.S, d.S), d.S)
         ks = pl.ds(pl.multiple_of(g * d.K, d.K), d.K)
-        for b in range(d.NB):
-            lanes = slice(256 * b, 256 * b + 256)
-            j = g * d.NB + b
-            r.k2[ks, lanes] = tn(r.ds2[j], spread(r.q2[qs, lanes], hb2)).astype(BF)
-            r.v2[ks, lanes] = tn(r.p2[j], spread(r.do2[qs, lanes], hb2)).astype(BF)
+        j = g * d.NB
+        dk = [tn(r.ds2[j + k], spread(r.q2[qs, b], hb2)).astype(BF) for k, b in enumerate(blocks)]
+        dv = [tn(r.p2[j + k], spread(r.do2[qs, b], hb2)).astype(BF) for k, b in enumerate(blocks)]
+        for k, b in enumerate(blocks):
+            r.k2[ks, b] = dk[k]
+            r.v2[ks, b] = dv[k]
         return c
 
     lax.fori_loop(0, d.GO, cross_keys, 0)
-    pair = pl.ds(pl.multiple_of((mp // 2) * 2 * d.C, 128), 2 * d.C)
-
-    def split_columns(unit, away, lane, value):
-        left, right = value[:, : d.C], value[:, d.C :]
-        first = core == 0
-        unit.store(jnp.where(first, left, right), lane)
-        away.store(jnp.where(first, right, left), lane)
-
-    class Away:
-        def __init__(self, ref):
-            self.acc = ref
-
-        store = Unit.store
-
-    away1, away2 = Away(r.cs1), Away(r.cs2)
-    split_columns(units["c1"], away1, 0, tn(r.a2[...], r.dq2[:, pair]))
-    split_columns(units["c1"], away1, d.C, tn(r.c2[...], r.o2[:, pair]))
-    cc1 = send(r.cs1, r.cr1, sib)
     split_columns(units["c2"], away2, 0, tn(r.mem[...], r.k2[:, pair]))
-
-    def merge(unit, cp, got):
-        cp.wait_recv()
-        for j in range(d.nch):
-            unit.acc[j] = (unit.acc[j].astype(F32) + got[j].astype(F32)).astype(BF)
-        unit.go()
-
-    merge(units["c1"], cc1, r.cr1)
     split_columns(units["c2"], away2, d.C, tn(r.mem[...], r.v2[:, pair]))
     cc2 = send(r.cs2, r.cr2, sib)
-    steps("u1", "u2")
-
+    steps("d1", "d2")
     x3.wait_recv()
 
     def finish_out(i, c):
@@ -736,39 +775,42 @@
             return send(r.nst.at[k + 1], r.nrc.at[k + 1], devices[k + 1])
         return None
 
+    parts = 4
     base_r = state["r"]
-    state["r"] += d.GO
-
-    def memory_copy(g):
-        rows = pl.ds(pl.multiple_of(core * d.MO + g * d.K, 16), d.K)
-        return remote(r.memory_grad.at[rows], r.memory_grad.at[rows], sib, base_r + g)
-
-    def memory_group(g, c):
-        ks = pl.ds(pl.multiple_of(g * d.K, d.K), d.K)
-        value = nn(r.k2[ks, :], r.ck[...]) + nn(r.v2[ks, :], r.cv[...])
-        r.memory_grad[pl.ds(pl.multiple_of(core * d.MO + g * d.K, 16), d.K), :] = value.astype(BF)
-        memory_copy(g).start()
+    state["r"] += parts
+    piece_rows = d.MO // parts
+
+    def memory_copy(i):
+        rows = pl.ds(pl.multiple_of(core * d.MO + i * piece_rows, 16), piece_rows)
+        return remote(r.memory_grad.at[rows], r.memory_grad.at[rows], sib, base_r + i)
+
+    def memory_part(i, c):
+        s = pl.ds(pl.multiple_of(i * piece_rows, 16), piece_rows)
+        there = pl.ds(pl.multiple_of(core * d.MO + i * piece_rows, 16), piece_rows)
+        value = nn(r.k2[s, :], r.ck[...]) + nn(r.v2[s, :], r.cv[...])
+        r.memory_grad[there, :] = value.astype(BF)
+        memory_copy(i).start()
         return c
 
-    lax.fori_loop(0, d.GO, memory_group, 0)
+    lax.fori_loop(0, 2, memory_part, 0)
     ncp = norm_step(0, ncp)
-    steps("s1", "s2", "d1", "d2")
+    steps("s1", "u2", "c1", "u1")
+    lax.fori_loop(2, 4, memory_part, 0)
     k = 1
+    rounds = [("s2", "u2"), ("c1", "s1"), ("c2", "s2")]
     while ncp is not None:
         ncp = norm_step(k, ncp)
+        if rounds:
+            steps(*rounds.pop(0))
         k += 1
-        if k == 2:
-            steps("c1", "c2")
-        if k == 3:
-            steps("s1", "s2")
     r.norms[...] = r.nst[len(devices)]
-    order = ("d1", "d2", "u1", "u2", "s1", "s2", "c1", "c2")
+    order = ("d1", "d2", "u1", "u2", "s1", "c1", "s2", "c2")
     while any(units[u].stage < d.bits for u in order):
         for u in order:
             if units[u].stage < d.bits:
                 units[u].step()
-    for g in range(d.GO):
-        memory_copy(g).wait()
+    for i in range(parts):
+        memory_copy(i).wait()
     for cp in tail:
         cp.wait_recv()
     for cp in sends:

time: 127 us -> 109 us (0.86)
  Pallas kernels: 126 us -> 108 us
    pallas_call x1, Pallas kernels: 122 us -> 104 us  [on_device(): pl.pallas_call(body, out_shape=[pltpu.VMEM(*s) for s in shapes], in_specs...]
where the time goes in v3:
time: 109 us
  Pallas kernels  108 us (99%)
    pallas_call x1, Pallas kernels, on_device(): pl.pallas_call(body, out_shape=[pltpu.VMEM(*s) for s in shapes], in_specs...  104 us
    pallas_call x1, Pallas kernels, on_device(): pl.pallas_call(write, out_shape=[jax.ShapeDtypeStruct(*s) for s in shapes...  4.01 us

profile of v3, /device:TPU:0, one launch (start us, length us, event | category | flops | bytes accessed | tf_op | source)
XLA Modules:
  0.0 108.6 jit_solution(16918449348890138049)
XLA Ops:
  0.7 103.7 %layer.1 = (bf16[448,768]{1,0:T(8,128)(2,1)S(1)}, bf16[448,768]{1,0:T(8,128)(2,1)S(1)}, bf16[3584,768]{1,0:T(8,128)(2,1)S(1)}, f32[96,192]{1,0:T(8,128)S(1)}, f3...) custom-call(bf16[448,768]{1,0:T(8,128)(2,1)} %refs_0_.1, ...), custom_call_target="tpu_custom_call" | custom-call | tf_op jit(solution)/shard_map/layer/pallas_call | solution.py:852
  104.4 4.0 %write.1 = (bf16[448,768]{1,0:T(8,128)(2,1)}, bf16[448,768]{1,0:T(8,128)(2,1)}, bf16[3584,768]{1,0:T(8,128)(2,1)}, f32[96,192]{1,0:T(8,128)}, f32[96,192]{1,0:T(...) custom-call(bf16[448,768]{1,0:T(8,128)(2,1)S(1)} %get-tuple-element., ...), custom_call_target="tpu_custom_call" | custom-call | tf_op jit(solution)/shard_map/write/pallas_call | solution.py:880

commit v4 on v3

--- a/solution.py
+++ b/solution.py
@@ -15,8 +15,8 @@
 EPSILON = 1e-06
 NEG_FILL = -1e30
 UNIT = 384
+GP = 7
 ROWS = 112
-N_SEMS = 160
 VMEM_BYTES = 54 * 2**20
 
 
@@ -81,10 +81,12 @@
         self.halvings = halvings
         self.low = self.bits - halvings
         self.nch = 1 << halvings
+        self.copies = 44 + 10 * self.bits
         self.rp = self.D // self.nch
 
 
-UNITS = ("d1", "d2", "u1", "u2", "s1", "s2", "c1", "c2")
+UNITS = ("d1", "d2", "u1", "u2", "s1", "s2", "c1", "c2", "c3")
+FOLDED = ("c2", "c3")
 IN_NAMES = (
     "suffix",
     "memory",
@@ -109,6 +111,7 @@
     "mlp_up",
     "mlp_down",
 )
+COUNTS, GAINS = IN_NAMES[3:6], IN_NAMES[6:12]
 OUT_NAMES = (
     "layer_out",
     "suffix_grad",
@@ -168,20 +171,26 @@
     vmem("act", (T, F))
     vmem("du", (T, F))
     vmem("dact", (T, F), F32)
-    for n in ("cs1", "cs2", "cr1", "cr2"):
-        vmem(n, (d.nch, d.rp, UNIT))
     for u in UNITS:
-        vmem("g_" + u + "_acc", (d.nch, d.rp, UNIT))
+        rows = d.rp // 2 if u in FOLDED else d.rp
+        vmem("g_" + u + "_acc", (d.nch, rows, UNIT))
+        if u[0] == "c":
+            vmem("g_" + u + "_away", (d.nch, rows, UNIT))
+            vmem("g_" + u + "_back", (d.nch, rows, UNIT))
         for k in range(d.halvings):
-            vmem(f"g_{u}_r{k}", (d.nch >> (k + 1), d.rp, UNIT))
+            vmem(f"g_{u}_r{k}", (d.nch >> (k + 1), rows, UNIT))
         for k in range(d.low):
-            vmem(f"g_{u}_x{k}", (d.rp, UNIT))
-            vmem(f"g_{u}_y{k}", (d.rp, UNIT))
+            vmem(f"g_{u}_x{k}", (rows, UNIT))
+            vmem(f"g_{u}_y{k}", (rows, UNIT))
     vmem("nst", (2 + d.bits, 8, D), F32)
     vmem("nrc", (1 + d.bits, 8, D), F32)
-    s["ss"] = pltpu.SemaphoreType.DMA((N_SEMS,))
-    s["rs"] = pltpu.SemaphoreType.DMA((N_SEMS,))
-    s["ls"] = pltpu.SemaphoreType.DMA((48,))
+    for n in GAINS:
+        s["v_" + n] = pltpu.VMEM((D,), F32)
+    for n in COUNTS:
+        s["n_" + n] = pltpu.SMEM((d.G,), jnp.int32)
+    s["ss"] = pltpu.SemaphoreType.DMA((d.copies,))
+    s["rs"] = pltpu.SemaphoreType.DMA((d.copies,))
+    s["ls"] = pltpu.SemaphoreType.DMA((22,))
     return s
 
 
@@ -239,27 +248,31 @@
         cp.start()
         return cp
 
+    barrier = pltpu.get_barrier_semaphore()
+    mates = [sib, xmate, corner] + [mate(b) for b in range(d.bits)]
+    for device in mates:
+        pl.semaphore_signal(barrier, inc=1, device_id=device, device_id_type=MESH)
     ld = {}
     mp_rows = pl.ds(pl.multiple_of(mp * d.C, 16), d.C)
+    ld["xin"] = load(r.suffix, r.xin)
+    for n in GAINS[:2]:
+        ld[n] = load(getattr(r, n), getattr(r, "v_" + n))
+    ld["sq"] = load(r.self_query, r.wqkv.at[pl.ds(0, d.C)])
+    ld["sk"] = load(r.self_key, r.wqkv.at[pl.ds(d.C, d.C)])
+    ld["sv"] = load(r.self_value, r.wqkv.at[pl.ds(2 * d.C, d.C)])
     ld["ck"] = load(r.cross_key, r.ck.at[mp_rows])
     ld["cv"] = load(r.cross_value, r.cv.at[mp_rows])
     ld["cq"] = load(r.cross_query, r.cq.at[mp_rows])
     ld["co"] = load(r.cross_out, r.co.at[mp_rows])
-    ld["xin"] = load(r.suffix, r.xin)
-    ld["sq"] = load(r.self_query, r.wqkv.at[pl.ds(0, d.C)])
-    ld["sk"] = load(r.self_key, r.wqkv.at[pl.ds(d.C, d.C)])
-    ld["sv"] = load(r.self_value, r.wqkv.at[pl.ds(2 * d.C, d.C)])
+    for n in COUNTS:
+        ld[n] = load(getattr(r, n), getattr(r, "n_" + n))
+    for n in GAINS[2:]:
+        ld[n] = load(getattr(r, n), getattr(r, "v_" + n))
     ld["so"] = load(r.self_out, r.so)
     ld["cot"] = load(r.cotangent, r.cot)
     ld["dn"] = load(r.mlp_down, r.dn)
     ld["mem"] = load(r.memory.at[pl.ds(pl.multiple_of(core * d.MO, 16), d.MO)], r.mem)
     ld["up"] = load(r.mlp_up, r.up)
-
-    barrier = pltpu.get_barrier_semaphore()
-    mates = [sib, xmate, corner] + [mate(b) for b in range(d.bits)]
-    for device in mates:
-        pl.semaphore_signal(barrier, inc=1, device_id=device, device_id_type=MESH)
-    pl.semaphore_wait(barrier, len(mates))
 
     PC = d.C // 4
     piece = lax.rem(dp, 4)
@@ -293,33 +306,56 @@
         gat[w, "s"].wait_recv()
         gat[w, "f"].wait_recv()
 
-    for w in ("ck", "cv", "cq", "co"):
-        gather_start(w)
 
     class Unit:
-        def __init__(self, name, finish, swap=False):
+        def __init__(self, name, finish, flip=0):
             self.name, self.finish, self.stage = name, finish, 0
-            self.order = list(range(d.halvings))
-            if swap:
-                self.order[:2] = 1, 0
+            self.flip = flip
             self.acc = getattr(r, f"g_{name}_acc")
             self.base = 0
             self.cp = None
 
-        def store(self, value, lane):
+        def store(self, value, lane, acc=None):
+            flip = self.flip
+            if acc is None:
+                acc = self.acc
+            elif not isinstance(flip, int):
+                flip = 1 - flip
             width = value.shape[1]
+            half = d.rp // 2
             for j in range(d.nch):
-                p = sum(((j >> b) & 1) * (d.nch >> (k + 1)) for k, b in enumerate(self.order))
-                self.acc[p, :, lane : lane + width] = value[j * d.rp : (j + 1) * d.rp].astype(BF)
+                bits = [(j >> k) & 1 for k in range(d.halvings)]
+                size = [d.nch >> (k + 1) for k in range(d.halvings)]
+                p = sum(x * y for x, y in zip(bits, size))
+                p = p + flip * (bits[1] - bits[0]) * (size[0] - size[1])
+                part = value[j * d.rp : (j + 1) * d.rp].astype(BF)
+                if self.name in FOLDED:
+                    acc[p, :, :width] = part[:half]
+                    acc[p, :, width:] = part[half:]
+                else:
+                    acc[p, :, lane : lane + width] = part
+
+        def bit(self, k):
+            if k > 1:
+                return bit_of(d.low + k)
+            near, far = bit_of(d.low + k), bit_of(d.low + 1 - k)
+            return near + self.flip * (far - near)
+
+        def mate(self, k):
+            b = d.low + k
+            step = (1 << b) * (1 - 2 * bit_of(b))
+            if k < 2:
+                c = d.low + 1 - k
+                step = step + self.flip * ((1 << c) * (1 - 2 * bit_of(c)) - step)
+            return {"dp": dp + step}
 
         def go(self):
             k = self.stage
             if k < d.halvings:
                 half = d.nch >> (k + 1)
-                b = d.low + self.order[k]
                 dst = getattr(r, f"g_{self.name}_r{k}")
-                src = self.acc.at[pl.ds(self.base + (1 - bit_of(b)) * half, half)]
-                self.cp = send(src, dst, mate(b))
+                src = self.acc.at[pl.ds(self.base + (1 - self.bit(k)) * half, half)]
+                self.cp = send(src, dst, self.mate(k))
             else:
                 e = k - d.halvings
                 x = getattr(r, f"g_{self.name}_x{e}")
@@ -332,7 +368,7 @@
             if k < d.halvings:
                 half = d.nch >> (k + 1)
                 got = getattr(r, f"g_{self.name}_r{k}")
-                base = self.base + bit_of(d.low + self.order[k]) * half
+                base = self.base + self.bit(k) * half
                 self.base = base
                 if k < d.halvings - 1:
                     for j in range(half):
@@ -375,15 +411,24 @@
 
         return f
 
+    def fin_fold(ref):
+        def f(v):
+            ref[: d.rp // 2, :] = v[:, : d.C]
+            ref[d.rp // 2 :, :] = v[:, d.C :]
+
+        return f
+
+    turn = core
     units = {
-        "d1": Unit("d1", fin_dn(0)),
-        "d2": Unit("d2", fin_dn(UNIT), True),
-        "u1": Unit("u1", fin_up(0)),
-        "u2": Unit("u2", fin_up(UNIT)),
-        "s1": Unit("s1", fin_pair(r.g_sq, r.g_sk, False)),
-        "s2": Unit("s2", fin_pair(r.g_sv, r.g_so, True), True),
-        "c1": Unit("c1", fin_pair(r.g_cq, r.g_co, True)),
-        "c2": Unit("c2", fin_pair(r.g_ck, r.g_cv, False)),
+        "d1": Unit("d1", fin_dn(0), turn),
+        "d2": Unit("d2", fin_dn(UNIT), 1 - turn),
+        "u1": Unit("u1", fin_up(0), turn),
+        "u2": Unit("u2", fin_up(UNIT), 1 - turn),
+        "s1": Unit("s1", fin_pair(r.g_sq, r.g_sk, False), turn),
+        "s2": Unit("s2", fin_pair(r.g_sv, r.g_so, True), 1 - turn),
+        "c1": Unit("c1", fin_pair(r.g_cq, r.g_co, True), turn),
+        "c2": Unit("c2", fin_fold(r.g_ck), turn),
+        "c3": Unit("c3", fin_fold(r.g_cv), 1 - turn),
     }
 
     def steps(*which):
@@ -406,13 +451,12 @@
         return getattr(r, f"xs{k}")[s, :].astype(F32) + getattr(r, f"xr{k}")[s, :].astype(F32)
 
     def row_loop(n, body, carry=0):
-        def step(i, c):
-            return body(pl.multiple_of(i * ROWS, ROWS), c)
-
-        return lax.fori_loop(0, n // ROWS, step, carry)
-
-    def vec(ref):
-        return ref[...].reshape(1, d.D)
+        for i in range(0, n, ROWS):
+            carry = body(i, carry)
+        return carry
+
+    def vec(name):
+        return getattr(r, "v_" + name)[...].reshape(1, d.D)
 
     def head_masks(width, count):
         col = lax.broadcasted_iota(jnp.int32, (1, width), 1)
@@ -436,8 +480,9 @@
     for n in ("q1", "k1", "v1", "o1", "do1"):
         ref = getattr(r, n)
         ref[d.T :, :] = jnp.zeros((d.TP - d.T, d.C), BF)
-    ld["xin"].wait()
-    gain, shift = vec(r.gain_self), vec(r.shift_self)
+    for n in ("xin", *GAINS):
+        ld[n].wait()
+    gain, shift = vec("gain_self"), vec("shift_self")
 
     def norm_one(i, c):
         s = pl.ds(i, ROWS)
@@ -452,29 +497,42 @@
     r.q1[: d.T, :] = (qkv[:, : d.C] * factor).astype(BF)
     r.k1[: d.T, :] = qkv[:, d.C : 2 * d.C].astype(BF)
     r.v1[: d.T, :] = qkv[:, 2 * d.C :].astype(BF)
-    gather_x("ck")
+    for n in COUNTS:
+        ld[n].wait()
+    pl.semaphore_wait(barrier, len(mates))
+    for w in full:
+        gather_start(w)
 
     ri = lax.broadcasted_iota(jnp.int32, (128, 128), 0)
     ci = lax.broadcasted_iota(jnp.int32, (128, 128), 1)
     near = (jnp.right_shift(ri, 5) == jnp.right_shift(ci, 5)) & (ci <= ri)
     place = jnp.bitwise_and(ci, 31)
     per = 128 // d.S
+    tiles = [pl.ds(t * 128, 128) for t in range(d.BLK)]
+    okays = []
     for t in range(d.BLK):
         lens = jnp.zeros((128, 128), jnp.int32)
         for k in range(per):
             g = t * per + k
             if g < d.G:
-                lens = jnp.where(jnp.right_shift(ci, 5) == k, r.slen[g], lens)
-        ok = near & (place < lens)
-        b = pl.ds(t * 128, 128)
-        scores = nt(spread(r.q1[b, :], hb1), r.k1[b, :])
-        scores = jnp.concatenate(
-            [jnp.where(ok, scores[h * 128 : (h + 1) * 128], NEG_FILL) for h in range(HC)], axis=0
+                lens = jnp.where(jnp.right_shift(ci, 5) == k, r.n_slen[g], lens)
+        okays.append(near & (place < lens))
+    sc = [nt(spread(r.q1[b, :], hb1), r.k1[b, :]) for b in tiles]
+    sc = [
+        jnp.concatenate(
+            [jnp.where(ok, x[h * 128 : (h + 1) * 128], NEG_FILL) for h in range(HC)], axis=0
         )
-        p = softmax(scores).astype(BF)
-        r.p1[t] = p
-        r.o1[b, :] = gatherh(nn(p, r.v1[b, :]), hf1).astype(BF)
-    gather_x("cv")
+        for x, ok in zip(sc, okays)
+    ]
+    top = [jnp.max(x, axis=-1, keepdims=True) for x in sc]
+    sc = [jnp.exp(x - t) for x, t in zip(sc, top)]
+    inv = [1.0 / jnp.sum(x, axis=-1, keepdims=True) for x in sc]
+    sc = [(x * t).astype(BF) for x, t in zip(sc, inv)]
+    out = [nn(x, r.v1[b, :]) for x, b in zip(sc, tiles)]
+    for t, b in enumerate(tiles):
+        r.p1[t] = sc[t]
+        r.o1[b, :] = gatherh(out[t], hf1).astype(BF)
+    gather_x("ck")
     ld["so"].wait()
 
     def out_one(rows):
@@ -484,31 +542,36 @@
     ld["cot"].wait()
     ld["dn"].wait()
     r.dact[...] = nt(r.cot[...], r.dn[...])
+    gather_x("cv")
     x1 = reduce_end(1, out_one, x1)
 
     gather_x("cq")
-    gather_x("co")
-    gather_y("ck")
     ld["mem"].wait()
     big = d.MO // 2
-
-    def project(w, dst):
-        def body(i, c):
-            s = pl.ds(pl.multiple_of(i * big, 16), big)
-            dst[s, :] = nt(r.mem[s, :], w[...]).astype(BF)
-            return c
-
-        lax.fori_loop(0, 2, body, 0)
-
-    gather_done("ck")
-    project(r.ck, r.k2)
+    near_pair = pl.multiple_of((mp // 2) * 2 * d.C, 128)
+    far_pair = pl.multiple_of(2 * d.C - (mp // 2) * 2 * d.C, 128)
+
+    def project(w, dst, start):
+        cols = pl.ds(start, 2 * d.C)
+
+        for i in range(2):
+            s = pl.ds(i * big, big)
+            dst[s, cols] = nt(r.mem[s, :], w[cols, :]).astype(BF)
+
+    gat["ck", "s"].wait_recv()
+    project(r.ck, r.k2, near_pair)
+    gather_x("co")
+    gat["cv", "s"].wait_recv()
+    project(r.cv, r.v2, near_pair)
+    gather_y("ck")
+    gat["ck", "f"].wait_recv()
+    project(r.ck, r.k2, far_pair)
     gather_y("cv")
-    gather_done("cv")
-    project(r.cv, r.v2)
+    gat["cv", "f"].wait_recv()
+    project(r.cv, r.v2, far_pair)
     gather_y("cq")
-
     x1.wait_recv()
-    gain, shift = vec(r.gain_cross), vec(r.shift_cross)
+    gain, shift = vec("gain_cross"), vec("shift_cross")
 
     def norm_two(i, c):
         s = pl.ds(i, ROWS)
@@ -525,30 +588,36 @@
 
     blocks = [slice(256 * b, 256 * b + 256) for b in range(d.NB)]
 
-    def cross_forward(g, c):
-        n = core * d.GO + g
-        live = r.kind[n] * PATCHES + r.prefix[n]
-        qs = pl.ds(pl.multiple_of(g * d.S, d.S), d.S)
-        ks = pl.ds(pl.multiple_of(g * d.K, d.K), d.K)
-        v = [r.v2[ks, b] for b in blocks]
-        s = [nt(spread(r.q2[qs, b], hb2), r.k2[ks, b]) for b in blocks]
-        s = [jnp.where(slot < live, x, NEG_FILL) for x in s]
+    def over_groups(body):
+        for start in range(0, d.GO, GP):
+            body(range(start, min(start + GP, d.GO)))
+
+    def group_rows(g):
+        return pl.ds(g * d.S, d.S), pl.ds(g * d.K, d.K)
+
+    def cross_forward(groups):
+        todo = [(g, k, *group_rows(g), b) for g in groups for k, b in enumerate(blocks)]
+        n = [core * d.GO + g for g in groups]
+        live = [r.n_kind[i] * PATCHES + r.n_prefix[i] for i in n]
+        live = [x for x in live for b in blocks]
+        v = [r.v2[ks, b] for g, k, qs, ks, b in todo]
+        s = [nt(spread(r.q2[qs, b], hb2), r.k2[ks, b]) for g, k, qs, ks, b in todo]
+        s = [jnp.where(slot < m, x, NEG_FILL) for x, m in zip(s, live)]
         top = [jnp.max(x, axis=-1, keepdims=True) for x in s]
         p = [jnp.exp(x - t) for x, t in zip(s, top)]
         scale = [1.0 / jnp.sum(x, axis=-1, keepdims=True) for x in p]
         p = [(x * t).astype(BF) for x, t in zip(p, scale)]
         o = [nn(x, y) for x, y in zip(p, v)]
         o = [gatherh(x, hf2).astype(BF) for x in o]
-        for k, b in enumerate(blocks):
-            r.p2[g * d.NB + k] = p[k]
-            r.o2[qs, b] = o[k]
-        return c
-
-    lax.fori_loop(0, d.GO, cross_forward, 0)
+        for (g, k, qs, ks, b), x, y in zip(todo, p, o):
+            r.p2[g * d.NB + k] = x
+            r.o2[qs, b] = y
+
+    over_groups(cross_forward)
     gather_y("co")
     gather_done("co")
     r.tmp[...] = nn(r.o2[...], r.co[...])
-    gain, shift = vec(r.gain_mlp), vec(r.shift_mlp)
+    gain, shift = vec("gain_mlp"), vec("shift_mlp")
 
     def norm_three(i, c):
         s = pl.ds(i, ROWS)
@@ -600,8 +669,9 @@
         units[u].go()
     x3 = reduce_end(3, out_three, x3)
 
+    steps("d1", "d2")
     x4.wait_recv()
-    gain = vec(r.gain_mlp)
+    gain = vec("gain_mlp")
     zero8 = jnp.zeros((8, d.D), F32)
 
     def back_three(i, c):
@@ -619,27 +689,24 @@
     gain_mlp_grad, shift_mlp_grad = row_loop(d.RO, back_three, (zero8, zero8))
     r.do2[...] = nt(r.c2[...], r.co[...]).astype(BF)
 
-    def cross_backward(g, c):
-        qs = pl.ds(pl.multiple_of(g * d.S, d.S), d.S)
-        ks = pl.ds(pl.multiple_of(g * d.K, d.K), d.K)
-        k2 = [r.k2[ks, b] for b in blocks]
-        p = [r.p2[g * d.NB + k].astype(F32) for k in range(d.NB)]
-        t = [nt(spread(r.do2[qs, b], hb2), r.v2[ks, b]) for b in blocks]
+    def cross_backward(groups):
+        todo = [(g, k, *group_rows(g), b) for g in groups for k, b in enumerate(blocks)]
+        k2 = [r.k2[ks, b] for g, k, qs, ks, b in todo]
+        p = [r.p2[g * d.NB + k].astype(F32) for g, k, qs, ks, b in todo]
+        t = [nt(spread(r.do2[qs, b], hb2), r.v2[ks, b]) for g, k, qs, ks, b in todo]
         t = [x * y for x, y in zip(p, t)]
         centre = [jnp.sum(x, axis=-1, keepdims=True) for x in t]
         ds = [(x - y * m).astype(BF) for x, y, m in zip(t, p, centre)]
         dq = [nn(x, y) for x, y in zip(ds, k2)]
         dq = [(gatherh(x, hf2) * factor).astype(BF) for x in dq]
-        for k, b in enumerate(blocks):
-            r.ds2[g * d.NB + k] = ds[k]
-            r.dq2[qs, b] = dq[k]
-        return c
-
-    steps("d1", "d2")
-    lax.fori_loop(0, d.GO, cross_backward, 0)
+        for (g, k, qs, ks, b), x, y in zip(todo, ds, dq):
+            r.ds2[g * d.NB + k] = x
+            r.dq2[qs, b] = y
+
+    over_groups(cross_backward)
     r.tmp[...] = nn(r.dq2[...], r.cq[...])
-    steps("u1")
-    gain = vec(r.gain_cross)
+    steps("u1", "u2")
+    gain = vec("gain_cross")
 
     def back_two(i, c):
         gg, gs = c
@@ -655,47 +722,44 @@
     c1 = send(r.c1.at[own_rows], r.c1.at[own_rows], sib)
     pair = pl.ds(pl.multiple_of((mp // 2) * 2 * d.C, 128), 2 * d.C)
 
-    def split_columns(unit, away, lane, value):
+    def split_columns(u, lane, value):
         left, right = value[:, : d.C], value[:, d.C :]
         first = core == 0
-        unit.store(jnp.where(first, left, right), lane)
-        away.store(jnp.where(first, right, left), lane)
-
-    class Away:
-        def __init__(self, ref, order):
-            self.acc, self.order = ref, order
-
-        store = Unit.store
-
-    away1 = Away(r.cs1, units["c1"].order)
-    away2 = Away(r.cs2, units["c2"].order)
-    def merge(unit, cp, got):
+        units[u].store(jnp.where(first, left, right), lane)
+        units[u].store(jnp.where(first, right, left), lane, getattr(r, f"g_{u}_away"))
+
+    def swap(u):
+        return send(getattr(r, f"g_{u}_away"), getattr(r, f"g_{u}_back"), sib)
+
+    def merge(u, cp):
+        unit, got = units[u], getattr(r, f"g_{u}_back")
         cp.wait_recv()
         for j in range(d.nch):
             unit.acc[j] = (unit.acc[j].astype(F32) + got[j].astype(F32)).astype(BF)
         unit.go()
 
-    split_columns(units["c1"], away1, 0, tn(r.a2[...], r.dq2[:, pair]))
-    split_columns(units["c1"], away1, d.C, tn(r.c2[...], r.o2[:, pair]))
-    cc1 = send(r.cs1, r.cr1, sib)
+    split_columns("c1", 0, tn(r.a2[...], r.dq2[:, pair]))
+    split_columns("c1", d.C, tn(r.c2[...], r.o2[:, pair]))
+    cc1 = swap("c1")
     r.do1[own_rows, :] = nt(r.c1[own_rows, :], r.so[...]).astype(BF)
+    merge("c1", cc1)
     c1.wait_recv()
     r.do1[other_rows, :] = nt(r.c1[other_rows, :], r.so[...]).astype(BF)
-    for t in range(d.BLK):
-        b = pl.ds(t * 128, 128)
-        dom = spread(r.do1[b, :], hb1)
-        dp_ = nt(dom, r.v1[b, :])
-        pb = r.p1[t]
-        p = pb.astype(F32)
-        tt = p * dp_
-        ds = (tt - p * jnp.sum(tt, axis=-1, keepdims=True)).astype(BF)
-        dq = gatherh(nn(ds, r.k1[b, :]), hf1) * factor
-        dk = tn(ds, spread(r.q1[b, :], hb1))
-        dv = tn(pb, dom)
-        r.dqkv[b, : d.C] = dq.astype(BF)
-        r.dqkv[b, d.C : 2 * d.C] = dk.astype(BF)
-        r.dqkv[b, 2 * d.C :] = dv.astype(BF)
-    steps("d1", "d2")
+    steps("d2", "d1")
+    dom = [spread(r.do1[b, :], hb1) for b in tiles]
+    tt = [nt(x, r.v1[b, :]) for x, b in zip(dom, tiles)]
+    pb = [r.p1[t] for t in range(d.BLK)]
+    pf = [x.astype(F32) for x in pb]
+    tt = [x * y for x, y in zip(tt, pf)]
+    mid = [jnp.sum(x, axis=-1, keepdims=True) for x in tt]
+    ds = [(x - y * m).astype(BF) for x, y, m in zip(tt, pf, mid)]
+    dq = [nn(x, r.k1[b, :]) for x, b in zip(ds, tiles)]
+    dk = [tn(x, spread(r.q1[b, :], hb1)) for x, b in zip(ds, tiles)]
+    dv = [tn(x, y) for x, y in zip(pb, dom)]
+    for t, b in enumerate(tiles):
+        r.dqkv[b, : d.C] = (gatherh(dq[t], hf1) * factor).astype(BF)
+        r.dqkv[b, d.C : 2 * d.C] = dk[t].astype(BF)
+        r.dqkv[b, 2 * d.C :] = dv[t].astype(BF)
 
     def back_six(rows):
         return nn(r.dqkv[rows, :], r.wqkv[...])
@@ -708,25 +772,27 @@
     units["s2"].store(tn(r.a1[...], r.dqkv[rows, 2 * d.C :]), 0)
     units["s2"].store(tn(r.c1[...], r.o1[rows, :]), d.C)
     units["s2"].go()
-    merge(units["c1"], cc1, r.cr1)
+
+    def cross_keys(left, right, dst):
+        def body(groups):
+            todo = [(g, k, *group_rows(g), b) for g in groups for k, b in enumerate(blocks)]
+            out = [
+                tn(left[g * d.NB + k], spread(right[qs, b], hb2)).astype(BF)
+                for g, k, qs, ks, b in todo
+            ]
+            for (g, k, qs, ks, b), x in zip(todo, out):
+                dst[ks, b] = x
+
+        over_groups(body)
+
+    cross_keys(r.ds2, r.q2, r.k2)
+    split_columns("c2", 0, tn(r.mem[...], r.k2[:, pair]))
+    cc2 = swap("c2")
     steps("u2", "u1")
-
-    def cross_keys(g, c):
-        qs = pl.ds(pl.multiple_of(g * d.S, d.S), d.S)
-        ks = pl.ds(pl.multiple_of(g * d.K, d.K), d.K)
-        j = g * d.NB
-        dk = [tn(r.ds2[j + k], spread(r.q2[qs, b], hb2)).astype(BF) for k, b in enumerate(blocks)]
-        dv = [tn(r.p2[j + k], spread(r.do2[qs, b], hb2)).astype(BF) for k, b in enumerate(blocks)]
-        for k, b in enumerate(blocks):
-            r.k2[ks, b] = dk[k]
-            r.v2[ks, b] = dv[k]
-        return c
-
-    lax.fori_loop(0, d.GO, cross_keys, 0)
-    split_columns(units["c2"], away2, 0, tn(r.mem[...], r.k2[:, pair]))
-    split_columns(units["c2"], away2, d.C, tn(r.mem[...], r.v2[:, pair]))
-    cc2 = send(r.cs2, r.cr2, sib)
-    steps("d1", "d2")
+    cross_keys(r.p2, r.do2, r.v2)
+    merge("c2", cc2)
+    split_columns("c3", 0, tn(r.mem[...], r.v2[:, pair]))
+    cc3 = swap("c3")
     x3.wait_recv()
 
     def finish_out(i, c):
@@ -736,10 +802,11 @@
 
     row_loop(d.RO, finish_out)
     tail = [send(r.layer_out.at[own_rows], r.layer_out.at[own_rows], sib)]
-    merge(units["c2"], cc2, r.cr2)
+    merge("c3", cc3)
+    steps("d2", "c1", "d1")
 
     x6.wait_recv()
-    gain = vec(r.gain_self)
+    gain = vec("gain_self")
 
     def back_one(i, c):
         gg, gs = c
@@ -784,38 +851,39 @@
         rows = pl.ds(pl.multiple_of(core * d.MO + i * piece_rows, 16), piece_rows)
         return remote(r.memory_grad.at[rows], r.memory_grad.at[rows], sib, base_r + i)
 
-    def memory_part(i, c):
-        s = pl.ds(pl.multiple_of(i * piece_rows, 16), piece_rows)
+    def memory_part(i):
+        s = pl.ds(i * piece_rows, piece_rows)
         there = pl.ds(pl.multiple_of(core * d.MO + i * piece_rows, 16), piece_rows)
         value = nn(r.k2[s, :], r.ck[...]) + nn(r.v2[s, :], r.cv[...])
         r.memory_grad[there, :] = value.astype(BF)
         memory_copy(i).start()
-        return c
-
-    lax.fori_loop(0, 2, memory_part, 0)
+
+    memory_part(0)
+    memory_part(1)
+    steps("s1", "u2")
     ncp = norm_step(0, ncp)
-    steps("s1", "u2", "c1", "u1")
-    lax.fori_loop(2, 4, memory_part, 0)
-    k = 1
-    rounds = [("s2", "u2"), ("c1", "s1"), ("c2", "s2")]
+    memory_part(2)
+    memory_part(3)
+    ncp = norm_step(1, ncp)
+    k = 2
+    for u in ("u1", "c1", "s2", "s1", "c2", "c1", "c3", "s1", "s2", "c2", "c3", "s2", "c2", "c3"):
+        steps(u)
+        if u == "c2" and ncp is not None:
+            ncp = norm_step(k, ncp)
+            k += 1
     while ncp is not None:
         ncp = norm_step(k, ncp)
-        if rounds:
-            steps(*rounds.pop(0))
         k += 1
     r.norms[...] = r.nst[len(devices)]
-    order = ("d1", "d2", "u1", "u2", "s1", "c1", "s2", "c2")
-    while any(units[u].stage < d.bits for u in order):
-        for u in order:
-            if units[u].stage < d.bits:
-                units[u].step()
+    while any(unit.stage < d.bits for unit in units.values()):
+        steps(*units)
     for i in range(parts):
         memory_copy(i).wait()
     for cp in tail:
         cp.wait_recv()
     for cp in sends:
         cp.wait_send()
-    assert state["r"] <= N_SEMS
+    assert state["r"] == d.copies
 
 
 def solution(mesh):
@@ -844,7 +912,6 @@
             ((8, d.D), F32),
         ]
         hbm, vmem = pl.BlockSpec(memory_space=pl.ANY), pl.BlockSpec(memory_space=pltpu.VMEM)
-        smem = pl.BlockSpec(memory_space=pltpu.SMEM)
 
         def body(*refs):
             kernel(d, names, *refs)
@@ -852,7 +919,7 @@
         outs = pl.pallas_call(
             body,
             out_shape=[pltpu.VMEM(*s) for s in shapes],
-            in_specs=[hbm] * 3 + [smem] * 3 + [vmem] * 6 + [hbm] * 10,
+            in_specs=[hbm] * 22,
             out_specs=[vmem] * 14,
             scratch_shapes=list(scr.values()),
             compiler_params=pltpu.CompilerParams(
@@ -865,9 +932,10 @@
 
         def write(*refs):
             ins, norms, dst, vectors, sem = refs[:13], refs[13], refs[14:27], refs[27:33], refs[33]
-            copies = [
-                pltpu.make_async_copy(a, b, sem.at[k]) for k, (a, b) in enumerate(zip(ins, dst))
-            ]
+            cut = d.M // 8
+            pieces = [(ins[2].at[pl.ds(k * cut, cut)], dst[2].at[pl.ds(k * cut, cut)]) for k in range(8)]
+            pieces += [(a, b) for k, (a, b) in enumerate(zip(ins, dst)) if k != 2]
+            copies = [pltpu.make_async_copy(a, b, sem.at[k]) for k, (a, b) in enumerate(pieces)]
             for cp in copies:
                 cp.start()
             shift = lax.rem(d.D - lax.axis_index("dp") * rows, d.D)
@@ -883,7 +951,7 @@
             + [jax.ShapeDtypeStruct((rows,), F32)] * 6,
             in_specs=[vmem] * 14,
             out_specs=[hbm] * 13 + [vmem] * 6,
-            scratch_shapes=[pltpu.SemaphoreType.DMA((13,))],
+            scratch_shapes=[pltpu.SemaphoreType.DMA((20,))],
             compiler_params=pltpu.CompilerParams(vmem_limit_bytes=2**20),
             name="write",
         )(*outs)

time: 109 us -> 95.8 us (0.88)
  Pallas kernels: 108 us -> 94.8 us
    pallas_call x1, Pallas kernels: 104 us -> 90.8 us  [on_device(): pl.pallas_call(body, out_shape=[pltpu.VMEM(*s) for s in shapes], in_specs...]
where the time goes in v4:
time: 95.8 us; the launch traced here: 95.6 us
  Pallas kernels  94.8 us (99%)
    pallas_call x1, Pallas kernels, on_device(): pl.pallas_call(body, out_shape=[pltpu.VMEM(*s) for s in shapes], in_specs...  90.8 us
    pallas_call x1, Pallas kernels, on_device(): pl.pallas_call(write, out_shape=[jax.ShapeDtypeStruct(*s) for s in shapes...  4.01 us

profile of v4, /device:TPU:0, one launch (start us, length us, event | category | flops | bytes accessed | tf_op | source)
XLA Modules:
  0.0 95.6 jit_solution(12133750500789786933)
XLA Ops:
  0.7 90.8 %layer.1 = (bf16[448,768]{1,0:T(8,128)(2,1)S(1)}, bf16[448,768]{1,0:T(8,128)(2,1)S(1)}, bf16[3584,768]{1,0:T(8,128)(2,1)S(1)}, f32[96,192]{1,0:T(8,128)S(1)}, f3...) custom-call(bf16[448,768]{1,0:T(8,128)(2,1)} %refs_0_.1, ...), custom_call_target="tpu_custom_call" | custom-call | tf_op jit(solution)/shard_map/layer/pallas_call | solution.py:919
  91.4 4.0 %write.1 = (bf16[448,768]{1,0:T(8,128)(2,1)}, bf16[448,768]{1,0:T(8,128)(2,1)}, bf16[3584,768]{1,0:T(8,128)(2,1)}, f32[96,192]{1,0:T(8,128)}, f32[96,192]{1,0:T(...) custom-call(bf16[448,768]{1,0:T(8,128)(2,1)S(1)} %get-tuple-element., ...), custom_call_target="tpu_custom_call" | custom-call | tf_op jit(solution)/shard_map/write/pallas_call | solution.py:948

commit v5 on v4

--- a/solution.py
+++ b/solution.py
@@ -427,8 +427,8 @@
         "s1": Unit("s1", fin_pair(r.g_sq, r.g_sk, False), turn),
         "s2": Unit("s2", fin_pair(r.g_sv, r.g_so, True), 1 - turn),
         "c1": Unit("c1", fin_pair(r.g_cq, r.g_co, True), turn),
-        "c2": Unit("c2", fin_fold(r.g_ck), turn),
-        "c3": Unit("c3", fin_fold(r.g_cv), 1 - turn),
+        "c2": Unit("c2", fin_fold(r.g_ck), 0),
+        "c3": Unit("c3", fin_fold(r.g_cv), 0),
     }
 
     def steps(*which):

time: 95.8 us -> 93.6 us (0.977)
  the two profiles are of different devices: /device:TPU:0 before, /device:TPU:1 now
where the time goes in v5:
time: 93.6 us; the launch traced here: 93.5 us
  Pallas kernels  92.6 us (99%)
    pallas_call x1, Pallas kernels, on_device(): pl.pallas_call(body, out_shape=[pltpu.VMEM(*s) for s in shapes], in_specs...  88.6 us
    pallas_call x1, Pallas kernels, on_device(): pl.pallas_call(write, out_shape=[jax.ShapeDtypeStruct(*s) for s in shapes...  4.01 us

profile of v5, /device:TPU:1, one launch (start us, length us, event | category | flops | bytes accessed | tf_op | source)
XLA Modules:
  0.0 93.5 jit_solution(2973907471205689212)
XLA Ops:
  0.7 88.6 %layer.1 = (bf16[448,768]{1,0:T(8,128)(2,1)S(1)}, bf16[448,768]{1,0:T(8,128)(2,1)S(1)}, bf16[3584,768]{1,0:T(8,128)(2,1)S(1)}, f32[96,192]{1,0:T(8,128)S(1)}, f3...) custom-call(bf16[448,768]{1,0:T(8,128)(2,1)} %refs_0_.1, ...), custom_call_target="tpu_custom_call" | custom-call | tf_op jit(solution)/shard_map/layer/pallas_call | solution.py:919
  89.3 4.0 %write.1 = (bf16[448,768]{1,0:T(8,128)(2,1)}, bf16[448,768]{1,0:T(8,128)(2,1)}, bf16[3584,768]{1,0:T(8,128)(2,1)}, f32[96,192]{1,0:T(8,128)}, f32[96,192]{1,0:T(...) custom-call(bf16[448,768]{1,0:T(8,128)(2,1)S(1)} %get-tuple-element., ...), custom_call_target="tpu_custom_call" | custom-call | tf_op jit(solution)/shard_map/write/pallas_call | solution.py:948
